TPU v7x, 512 devices: a whole 4x8x8 slice. The times are simulated.
512 devices in a mesh: seq: 32 (over x, z_hi, core), team: 16 (over z_lo, y).
Axes of the slice: x: 4, y: 8, z: 8 (z_hi: 4, z_lo: 2; z = z_hi * 2 + z_lo), core: 2. Of those that a mesh axis runs over, the one named last changes fastest.
Arguments:
- tokens: bfloat16 [32768, 1024], P(('seq', 'team')), may hold values from -6 to 6
- norm_gain: float32 [1024], replicated, may hold values from 0.1 to 1.9
- w_qkv: bfloat16 [1024, 3072], P('team'), may hold values from -1 to 1
- block_lists: int32 [256, 8], P('seq'), may hold values from 0 to 255, as said below
- block_counts: int32 [256], P('seq'), may hold values from 1 to 8, as said below
Outputs:
- attended: bfloat16 [32768, 1024], P('seq', 'team')
Inputs may be any that keep to these rules, and one draw needn't show every extreme that they name: `block_lists`: each query tile's list holds 8 distinct key tiles; the first is the query tile itself, the others are tiles of other sequence shards (a shard holds 8 tiles). The lists of one shard's query tiles name at most 2 distinct tiles of any one other shard, and exactly 2 of at least one other shard. `block_counts`: the first query tile has 1 valid entry and the last has 8.
All inputs are finite; a program needn't handle non-finite values.
Results may differ from a plain program's by a relative error of at most 0.0083.
Values may be sent and summed in bfloat16 or wider, within the bound.
A program may use at most 64 MiB of HBM per device.

v0:
```python
import jax
import jax.numpy as jnp
from jax import lax
from jax.sharding import PartitionSpec as P

HEADS = 16
HD = 64
TILE = 128
MAXB = 8


def passed_along(block, axis, distance):
    devices = range(lax.axis_size(axis))
    route = [((i - distance) % len(devices), i) for i in devices]
    return lax.ppermute(block, axis, route)


def on_device(tokens, norm_gain, w_qkv, block_lists, block_counts):
    xf = tokens.astype(jnp.float32)
    normed = (xf * lax.rsqrt(jnp.mean(xf * xf, axis=-1, keepdims=True) + 1e-05) * norm_gain).astype(
        jnp.bfloat16
    )
    teams = lax.axis_size("team")
    local_heads = HEADS // teams
    mixed = jnp.dot(
        normed,
        lax.all_gather(w_qkv, "team", axis=0, tiled=True),
        preferred_element_type=jnp.float32,
    )
    packed = mixed.astype(jnp.bfloat16).reshape(normed.shape[0], HEADS, 3 * HD)
    qkv = lax.all_to_all(packed, "team", split_axis=1, concat_axis=0, tiled=True)
    query = qkv[:, :, :HD]
    pairs = qkv[:, :, HD:]
    seq_rows = qkv.shape[0]
    shard_tiles = seq_rows // TILE
    valid = jnp.arange(MAXB, dtype=jnp.int32)[None, :] < block_counts[:, None]
    scale = HD ** (-0.5)

    def run_pairs(state, here, source, tiles):
        flat_mask = here.reshape(-1)
        total_pairs = flat_mask.shape[0]
        pair_count = jnp.sum(flat_mask.astype(jnp.int32))
        pair_order = jnp.argsort(
            jnp.where(flat_mask, 0, total_pairs) + jnp.arange(total_pairs, dtype=jnp.int32)
        )
        flat_source = source.reshape(-1)

        def one_pair(turn, state):
            best, total, accum = state
            pair_index = pair_order[turn]
            row_start = pair_index // MAXB * TILE
            key_value = lax.dynamic_index_in_dim(tiles, flat_source[pair_index], 0, keepdims=False)
            query_rows = lax.dynamic_slice_in_dim(query, row_start, TILE, 0)
            scores = (
                jnp.einsum(
                    "qhd,khd->hqk",
                    query_rows,
                    key_value[:, :, :HD],
                    preferred_element_type=jnp.float32,
                )
                * scale
            )
            old_best = lax.dynamic_slice_in_dim(best, row_start, TILE, 1)
            old_total = lax.dynamic_slice_in_dim(total, row_start, TILE, 1)
            old_accum = lax.dynamic_slice_in_dim(accum, row_start, TILE, 1)
            fresh = jnp.maximum(old_best, jnp.max(scores, axis=-1))
            weights = jnp.exp(scores - fresh[:, :, None])
            factor = jnp.exp(old_best - fresh)
            new_total = old_total * factor + jnp.sum(weights, axis=-1)
            new_accum = old_accum * factor[:, :, None] + jnp.einsum(
                "hqk,khd->hqd",
                weights.astype(jnp.bfloat16),
                key_value[:, :, HD:],
                preferred_element_type=jnp.float32,
            )
            best = lax.dynamic_update_slice_in_dim(best, fresh, row_start, 1)
            total = lax.dynamic_update_slice_in_dim(total, new_total, row_start, 1)
            accum = lax.dynamic_update_slice_in_dim(accum, new_accum, row_start, 1)
            return (best, total, accum)

        return lax.fori_loop(0, pair_count, one_pair, state)

    def update_piece(state, piece, first_tile):
        key_tiles = piece.shape[0] // TILE
        relative = block_lists - first_tile
        here = valid & (relative >= 0) & (relative < key_tiles)
        source = jnp.clip(relative, 0, key_tiles - 1)
        tiles = piece.reshape(key_tiles, TILE, local_heads, 2 * HD)
        return run_pairs(state, here, source, tiles)

    start_state = (
        jnp.full((local_heads, seq_rows), -1e30, jnp.float32),
        jnp.zeros((local_heads, seq_rows), jnp.float32),
        jnp.zeros((local_heads, seq_rows, HD), jnp.float32),
    )
    position = lax.axis_index("seq")
    shards = lax.axis_size("seq")

    def one_step(step, carry):
        state, piece = carry
        holder = (position - step) % shards
        state = update_piece(state, piece, holder * shard_tiles)
        piece = passed_along(piece, "seq", 1)
        return (state, piece)

    state, piece = lax.fori_loop(0, shards - 1, one_step, (start_state, pairs))
    holder = (position - (shards - 1)) % shards
    state = update_piece(state, piece, holder * shard_tiles)
    best, total, accum = state
    result = accum / total[:, :, None]
    return jnp.transpose(result, (1, 0, 2)).reshape(seq_rows, local_heads * HD).astype(jnp.bfloat16)


def solution(mesh):
    in_specs = (P(("seq", "team"), None), P(), P("team", None), P("seq", None), P("seq"))
    out_specs = P("seq", "team")
    return jax.shard_map(
        on_device, mesh=mesh, in_specs=in_specs, out_specs=out_specs, check_vma=False
    )
```

profile of v0, /device:TPU:461, one launch (start us, length us, event | category | flops | bytes accessed | tf_op | source)
XLA Modules:
  0.0 747.8 jit_solution(11276730121306804282)
XLA Ops:
  8.3 80.1 %all-gather.2.cloned.1.call-done = bf16[1024,3072]{1,0:T(8,128)(2,1)} async-done(((bf16[64,3072]{1,0:T(8,128)(2,1)}), bf16[1024,3072]{1,0:T(8,128)(2,1)}) %all-gather.2.cloned.1.call-update) | async-done | bytes 6291472 | tf_op jit(solution)/shard_map/all_gather | solution.py:27
  88.4 4.1 convolution_convert_fusion
  94.2 6.7 all-to-all-start
  101.1 2.1 sort.43
  104.0 10.5 %all-to-all-done = bf16[64,16,192]{2,0,1:T(8,128)(2,1)S(1)} async-done(((bf16[64,16,192]{2,0,1:T(8,128)(2,1)}), bf16[64,16,192]{2,0,1:T(8,128)(2,1)S(1)}, u32[]{:S(2)}, u32[]{:S(2)}) %all-to-all-start) | async-done | bytes 393248 | tf_op jit(solution)/shard_map/all_to_all | solution.py:31
  114.8 615.9 %while.75 = (s32[]{:T(128)}, f32[1,1024]{1,0:T(1,128)S(1)}, f32[1,1024]{1,0:T(1,128)S(1)}, f32[1,1024,64]{1,2,0:T(8,128)S(1)}, bf16[1024,1,128]{2,0,1:T(8,128)(2...) while((s32[]{:T(128)}, f32[1,1024]{1,0:T(1,128)S(1)}, ...), condition=%wide.region_8.9_spmd.clone, body=%wide.region_1.8_spmd.clone.sunk | while | flops 4310507 | bytes 1994932 | solution.py:106
  115.6 5.6 collective-permute-start
  122.2 2.0 sort.46
  124.2 64.4 %while.76 = (s32[]{:T(128)}, f32[1,1024]{1,0:T(1,128)S(1)}, f32[1,1024]{1,0:T(1,128)S(1)}, f32[1,1024,64]{1,2,0:T(8,128)S(1)}, s32[]{:T(128)}, /*index=5*/s32[64...) while((s32[]{:T(128)}, f32[1,1024]{1,0:T(1,128)S(1)}, ...), condition=%wide.region_7.7_spmd, body=%wide.region_4.6_spmd.sunk | while | flops 4309405 | bytes 417786 | solution.py:81
  192.2 2.0 sort.46
  194.8 2.5 collective-permute-done
  198.0 10.2 %collective-permute-start = (bf16[1024,1,128]{2,0,1:T(8,128)(2,1)}, bf16[1024,1,128]{2,0,1:T(8,128)(2,1)S(1)}, u32[]{:S(2)}, u32[]{:S(2)}) collective-permute-start(bf16[1024,1,128]{2,0,1:T(8,128)(2,1)} %copy.41), channel_id=1, source_target_pairs={{496,0},{0,16},{16,32},{32,48},{48,64},{64,80},{80,96},{96,112},{1... | collective-permute-start | bytes 786440 | tf_op jit(solution)/shard_map/while/body/eval_jaxpr/ppermute | solution.py:15
  209.2 2.0 sort.46
  211.2 16.6 %while.76 = (s32[]{:T(128)}, f32[1,1024]{1,0:T(1,128)S(1)}, f32[1,1024]{1,0:T(1,128)S(1)}, f32[1,1024,64]{1,2,0:T(8,128)S(1)}, s32[]{:T(128)}, /*index=5*/s32[64...) while((s32[]{:T(128)}, f32[1,1024]{1,0:T(1,128)S(1)}, ...), condition=%wide.region_7.7_spmd, body=%wide.region_4.6_spmd.sunk | while | flops 4309405 | bytes 417786 | solution.py:81
  231.4 2.0 sort.46
  234.0 2.7 collective-permute-done
  237.4 7.3 collective-permute-start
  245.7 2.0 sort.46
  250.6 8.4 %collective-permute-start = (bf16[1024,1,128]{2,0,1:T(8,128)(2,1)}, bf16[1024,1,128]{2,0,1:T(8,128)(2,1)S(1)}, u32[]{:S(2)}, u32[]{:S(2)}) collective-permute-start(bf16[1024,1,128]{2,0,1:T(8,128)(2,1)} %copy.41), channel_id=1, source_target_pairs={{496,0},{0,16},{16,32},{32,48},{48,64},{64,80},{80,96},{96,112},{1... | collective-permute-start | bytes 786440 | tf_op jit(solution)/shard_map/while/body/eval_jaxpr/ppermute | solution.py:15
  259.9 2.0 sort.46
  261.9 8.6 %while.76 = (s32[]{:T(128)}, f32[1,1024]{1,0:T(1,128)S(1)}, f32[1,1024]{1,0:T(1,128)S(1)}, f32[1,1024,64]{1,2,0:T(8,128)S(1)}, s32[]{:T(128)}, /*index=5*/s32[64...) while((s32[]{:T(128)}, f32[1,1024]{1,0:T(1,128)S(1)}, ...), condition=%wide.region_7.7_spmd, body=%wide.region_4.6_spmd.sunk | while | flops 4309405 | bytes 417786 | solution.py:81
  274.1 2.0 sort.46
  276.1 8.6 %while.76 = (s32[]{:T(128)}, f32[1,1024]{1,0:T(1,128)S(1)}, f32[1,1024]{1,0:T(1,128)S(1)}, f32[1,1024,64]{1,2,0:T(8,128)S(1)}, s32[]{:T(128)}, /*index=5*/s32[64...) while((s32[]{:T(128)}, f32[1,1024]{1,0:T(1,128)S(1)}, ...), condition=%wide.region_7.7_spmd, body=%wide.region_4.6_spmd.sunk | while | flops 4309405 | bytes 417786 | solution.py:81
  285.4 20.7 %collective-permute-start = (bf16[1024,1,128]{2,0,1:T(8,128)(2,1)}, bf16[1024,1,128]{2,0,1:T(8,128)(2,1)S(1)}, u32[]{:S(2)}, u32[]{:S(2)}) collective-permute-start(bf16[1024,1,128]{2,0,1:T(8,128)(2,1)} %copy.41), channel_id=1, source_target_pairs={{496,0},{0,16},{16,32},{32,48},{48,64},{64,80},{80,96},{96,112},{1... | collective-permute-start | bytes 786440 | tf_op jit(solution)/shard_map/while/body/eval_jaxpr/ppermute | solution.py:15
  307.1 2.0 sort.46
  309.1 16.6 %while.76 = (s32[]{:T(128)}, f32[1,1024]{1,0:T(1,128)S(1)}, f32[1,1024]{1,0:T(1,128)S(1)}, f32[1,1024,64]{1,2,0:T(8,128)S(1)}, s32[]{:T(128)}, /*index=5*/s32[64...) while((s32[]{:T(128)}, f32[1,1024]{1,0:T(1,128)S(1)}, ...), condition=%wide.region_7.7_spmd, body=%wide.region_4.6_spmd.sunk | while | flops 4309405 | bytes 417786 | solution.py:81
  329.2 2.0 sort.46
  331.9 2.6 collective-permute-done
  335.2 7.3 collective-permute-start
  343.5 2.0 sort.46
  345.5 8.6 %while.76 = (s32[]{:T(128)}, f32[1,1024]{1,0:T(1,128)S(1)}, f32[1,1024]{1,0:T(1,128)S(1)}, f32[1,1024,64]{1,2,0:T(8,128)S(1)}, s32[]{:T(128)}, /*index=5*/s32[64...) while((s32[]{:T(128)}, f32[1,1024]{1,0:T(1,128)S(1)}, ...), condition=%wide.region_7.7_spmd, body=%wide.region_4.6_spmd.sunk | while | flops 4309405 | bytes 417786 | solution.py:81
  357.7 2.0 sort.46
  360.4 2.5 collective-permute-done
  363.5 7.4 collective-permute-start
  371.9 2.0 sort.46
  373.9 8.6 %while.76 = (s32[]{:T(128)}, f32[1,1024]{1,0:T(1,128)S(1)}, f32[1,1024]{1,0:T(1,128)S(1)}, f32[1,1024,64]{1,2,0:T(8,128)S(1)}, s32[]{:T(128)}, /*index=5*/s32[64...) while((s32[]{:T(128)}, f32[1,1024]{1,0:T(1,128)S(1)}, ...), condition=%wide.region_7.7_spmd, body=%wide.region_4.6_spmd.sunk | while | flops 4309405 | bytes 417786 | solution.py:81
  386.1 2.0 sort.46
  388.1 16.6 %while.76 = (s32[]{:T(128)}, f32[1,1024]{1,0:T(1,128)S(1)}, f32[1,1024]{1,0:T(1,128)S(1)}, f32[1,1024,64]{1,2,0:T(8,128)S(1)}, s32[]{:T(128)}, /*index=5*/s32[64...) while((s32[]{:T(128)}, f32[1,1024]{1,0:T(1,128)S(1)}, ...), condition=%wide.region_7.7_spmd, body=%wide.region_4.6_spmd.sunk | while | flops 4309405 | bytes 417786 | solution.py:81
  408.3 2.0 sort.46
  410.3 8.6 %while.76 = (s32[]{:T(128)}, f32[1,1024]{1,0:T(1,128)S(1)}, f32[1,1024]{1,0:T(1,128)S(1)}, f32[1,1024,64]{1,2,0:T(8,128)S(1)}, s32[]{:T(128)}, /*index=5*/s32[64...) while((s32[]{:T(128)}, f32[1,1024]{1,0:T(1,128)S(1)}, ...), condition=%wide.region_7.7_spmd, body=%wide.region_4.6_spmd.sunk | while | flops 4309405 | bytes 417786 | solution.py:81
  419.6 15.5 %collective-permute-start = (bf16[1024,1,128]{2,0,1:T(8,128)(2,1)}, bf16[1024,1,128]{2,0,1:T(8,128)(2,1)S(1)}, u32[]{:S(2)}, u32[]{:S(2)}) collective-permute-start(bf16[1024,1,128]{2,0,1:T(8,128)(2,1)} %copy.41), channel_id=1, source_target_pairs={{496,0},{0,16},{16,32},{32,48},{48,64},{64,80},{80,96},{96,112},{1... | collective-permute-start | bytes 786440 | tf_op jit(solution)/shard_map/while/body/eval_jaxpr/ppermute | solution.py:15
  436.1 2.0 sort.46
  438.1 8.6 %while.76 = (s32[]{:T(128)}, f32[1,1024]{1,0:T(1,128)S(1)}, f32[1,1024]{1,0:T(1,128)S(1)}, f32[1,1024,64]{1,2,0:T(8,128)S(1)}, s32[]{:T(128)}, /*index=5*/s32[64...) while((s32[]{:T(128)}, f32[1,1024]{1,0:T(1,128)S(1)}, ...), condition=%wide.region_7.7_spmd, body=%wide.region_4.6_spmd.sunk | while | flops 4309405 | bytes 417786 | solution.py:81
  450.3 2.0 sort.46
  454.8 8.7 %collective-permute-start = (bf16[1024,1,128]{2,0,1:T(8,128)(2,1)}, bf16[1024,1,128]{2,0,1:T(8,128)(2,1)S(1)}, u32[]{:S(2)}, u32[]{:S(2)}) collective-permute-start(bf16[1024,1,128]{2,0,1:T(8,128)(2,1)} %copy.41), channel_id=1, source_target_pairs={{496,0},{0,16},{16,32},{32,48},{48,64},{64,80},{80,96},{96,112},{1... | collective-permute-start | bytes 786440 | tf_op jit(solution)/shard_map/while/body/eval_jaxpr/ppermute | solution.py:15
  466.5 8.6 %while.76 = (s32[]{:T(128)}, f32[1,1024]{1,0:T(1,128)S(1)}, f32[1,1024]{1,0:T(1,128)S(1)}, f32[1,1024,64]{1,2,0:T(8,128)S(1)}, s32[]{:T(128)}, /*index=5*/s32[64...) while((s32[]{:T(128)}, f32[1,1024]{1,0:T(1,128)S(1)}, ...), condition=%wide.region_7.7_spmd, body=%wide.region_4.6_spmd.sunk | while | flops 4309405 | bytes 417786 | solution.py:81
  480.7 8.6 %while.76 = (s32[]{:T(128)}, f32[1,1024]{1,0:T(1,128)S(1)}, f32[1,1024]{1,0:T(1,128)S(1)}, f32[1,1024,64]{1,2,0:T(8,128)S(1)}, s32[]{:T(128)}, /*index=5*/s32[64...) while((s32[]{:T(128)}, f32[1,1024]{1,0:T(1,128)S(1)}, ...), condition=%wide.region_7.7_spmd, body=%wide.region_4.6_spmd.sunk | while | flops 4309405 | bytes 417786 | solution.py:81
  494.9 8.6 %while.76 = (s32[]{:T(128)}, f32[1,1024]{1,0:T(1,128)S(1)}, f32[1,1024]{1,0:T(1,128)S(1)}, f32[1,1024,64]{1,2,0:T(8,128)S(1)}, s32[]{:T(128)}, /*index=5*/s32[64...) while((s32[]{:T(128)}, f32[1,1024]{1,0:T(1,128)S(1)}, ...), condition=%wide.region_7.7_spmd, body=%wide.region_4.6_spmd.sunk | while | flops 4309405 | bytes 417786 | solution.py:81
  509.1 8.6 %while.76 = (s32[]{:T(128)}, f32[1,1024]{1,0:T(1,128)S(1)}, f32[1,1024]{1,0:T(1,128)S(1)}, f32[1,1024,64]{1,2,0:T(8,128)S(1)}, s32[]{:T(128)}, /*index=5*/s32[64...) while((s32[]{:T(128)}, f32[1,1024]{1,0:T(1,128)S(1)}, ...), condition=%wide.region_7.7_spmd, body=%wide.region_4.6_spmd.sunk | while | flops 4309405 | bytes 417786 | solution.py:81
  523.3 8.6 %while.76 = (s32[]{:T(128)}, f32[1,1024]{1,0:T(1,128)S(1)}, f32[1,1024]{1,0:T(1,128)S(1)}, f32[1,1024,64]{1,2,0:T(8,128)S(1)}, s32[]{:T(128)}, /*index=5*/s32[64...) while((s32[]{:T(128)}, f32[1,1024]{1,0:T(1,128)S(1)}, ...), condition=%wide.region_7.7_spmd, body=%wide.region_4.6_spmd.sunk | while | flops 4309405 | bytes 417786 | solution.py:81
  537.5 8.6 %while.76 = (s32[]{:T(128)}, f32[1,1024]{1,0:T(1,128)S(1)}, f32[1,1024]{1,0:T(1,128)S(1)}, f32[1,1024,64]{1,2,0:T(8,128)S(1)}, s32[]{:T(128)}, /*index=5*/s32[64...) while((s32[]{:T(128)}, f32[1,1024]{1,0:T(1,128)S(1)}, ...), condition=%wide.region_7.7_spmd, body=%wide.region_4.6_spmd.sunk | while | flops 4309405 | bytes 417786 | solution.py:81
  551.7 8.6 %while.76 = (s32[]{:T(128)}, f32[1,1024]{1,0:T(1,128)S(1)}, f32[1,1024]{1,0:T(1,128)S(1)}, f32[1,1024,64]{1,2,0:T(8,128)S(1)}, s32[]{:T(128)}, /*index=5*/s32[64...) while((s32[]{:T(128)}, f32[1,1024]{1,0:T(1,128)S(1)}, ...), condition=%wide.region_7.7_spmd, body=%wide.region_4.6_spmd.sunk | while | flops 4309405 | bytes 417786 | solution.py:81
  561.1 4.8 collective-permute-start
  571.8 16.2 %collective-permute-start = (bf16[1024,1,128]{2,0,1:T(8,128)(2,1)}, bf16[1024,1,128]{2,0,1:T(8,128)(2,1)S(1)}, u32[]{:S(2)}, u32[]{:S(2)}) collective-permute-start(bf16[1024,1,128]{2,0,1:T(8,128)(2,1)} %copy.41), channel_id=1, source_target_pairs={{496,0},{0,16},{16,32},{32,48},{48,64},{64,80},{80,96},{96,112},{1... | collective-permute-start | bytes 786440 | tf_op jit(solution)/shard_map/while/body/eval_jaxpr/ppermute | solution.py:15
  591.0 16.6 %while.76 = (s32[]{:T(128)}, f32[1,1024]{1,0:T(1,128)S(1)}, f32[1,1024]{1,0:T(1,128)S(1)}, f32[1,1024,64]{1,2,0:T(8,128)S(1)}, s32[]{:T(128)}, /*index=5*/s32[64...) while((s32[]{:T(128)}, f32[1,1024]{1,0:T(1,128)S(1)}, ...), condition=%wide.region_7.7_spmd, body=%wide.region_4.6_spmd.sunk | while | flops 4309405 | bytes 417786 | solution.py:81
  616.0 7.3 collective-permute-start
  626.9 7.2 collective-permute-done
  640.3 4.9 collective-permute-done
  645.8 4.1 collective-permute-start
  652.9 16.6 %while.76 = (s32[]{:T(128)}, f32[1,1024]{1,0:T(1,128)S(1)}, f32[1,1024]{1,0:T(1,128)S(1)}, f32[1,1024,64]{1,2,0:T(8,128)S(1)}, s32[]{:T(128)}, /*index=5*/s32[64...) while((s32[]{:T(128)}, f32[1,1024]{1,0:T(1,128)S(1)}, ...), condition=%wide.region_7.7_spmd, body=%wide.region_4.6_spmd.sunk | while | flops 4309405 | bytes 417786 | solution.py:81
  670.2 18.8 %collective-permute-start = (bf16[1024,1,128]{2,0,1:T(8,128)(2,1)}, bf16[1024,1,128]{2,0,1:T(8,128)(2,1)S(1)}, u32[]{:S(2)}, u32[]{:S(2)}) collective-permute-start(bf16[1024,1,128]{2,0,1:T(8,128)(2,1)} %copy.41), channel_id=1, source_target_pairs={{496,0},{0,16},{16,32},{32,48},{48,64},{64,80},{80,96},{96,112},{1... | collective-permute-start | bytes 786440 | tf_op jit(solution)/shard_map/while/body/eval_jaxpr/ppermute | solution.py:15
  692.0 16.6 %while.76 = (s32[]{:T(128)}, f32[1,1024]{1,0:T(1,128)S(1)}, f32[1,1024]{1,0:T(1,128)S(1)}, f32[1,1024,64]{1,2,0:T(8,128)S(1)}, s32[]{:T(128)}, /*index=5*/s32[64...) while((s32[]{:T(128)}, f32[1,1024]{1,0:T(1,128)S(1)}, ...), condition=%wide.region_7.7_spmd, body=%wide.region_4.6_spmd.sunk | while | flops 4309405 | bytes 417786 | solution.py:81
  714.1 16.6 %while.76 = (s32[]{:T(128)}, f32[1,1024]{1,0:T(1,128)S(1)}, f32[1,1024]{1,0:T(1,128)S(1)}, f32[1,1024,64]{1,2,0:T(8,128)S(1)}, s32[]{:T(128)}, /*index=5*/s32[64...) while((s32[]{:T(128)}, f32[1,1024]{1,0:T(1,128)S(1)}, ...), condition=%wide.region_7.7_spmd, body=%wide.region_4.6_spmd.sunk | while | flops 4309405 | bytes 417786 | solution.py:81
  730.7 9.5 %while.73 = (s32[]{:T(128)}, f32[1,1024]{1,0:T(1,128)S(1)}, f32[1,1024]{1,0:T(1,128)S(1)}, f32[1,1024,64]{1,2,0:T(8,128)S(1)}, s32[]{:T(128)}, /*index=5*/s32[64...) while((s32[]{:T(128)}, f32[1,1024]{1,0:T(1,128)S(1)}, ...), condition=%wide.region_14.15_spmd, body=%wide.region_11.14_spmd.sunk | while | flops 4309405 | bytes 417786 | solution.py:81
  (595 shorter events, 215.4 us)
Async XLA Ops:
  6.5 94.3 %copy-start.1 = (s32[8]{0:T(128)S(1)}, s32[8]{0:T(128)}, u32[]{:S(2)}) copy-start(s32[8]{0:T(128)} %param.15) | copy-start | bytes 100
  6.5 94.3 %copy-start = (s32[8,8]{1,0:T(8,128)S(1)}, s32[8,8]{1,0:T(8,128)}, u32[]{:S(2)}) copy-start(s32[8,8]{1,0:T(8,128)} %param.14) | copy-start | bytes 772
  6.5 81.9 %all-gather.2.cloned.1.call-start = ((), (), s32[]{:S(2)}) async-start(), calls=%async_computation.1 | async-start | bytes 6684672 | tf_op jit(solution)/shard_map/all_gather | solution.py:27
  94.2 20.3 %all-to-all-start = ((bf16[64,16,192]{2,0,1:T(8,128)(2,1)}), bf16[64,16,192]{2,0,1:T(8,128)(2,1)S(1)}, u32[]{:S(2)}, u32[]{:S(2)}) async-start(bf16[64,16,192]{2,0,1:T(8,128)(2,1)} %copy.10), calls=%async_computation | async-start | bytes 1048576 | tf_op jit(solution)/shard_map/all_to_all | solution.py:31
  115.6 73.0 %collective-permute-start = (bf16[1024,1,128]{2,0,1:T(8,128)(2,1)}, bf16[1024,1,128]{2,0,1:T(8,128)(2,1)S(1)}, u32[]{:S(2)}, u32[]{:S(2)}) collective-permute-start(bf16[1024,1,128]{2,0,1:T(8,128)(2,1)} %copy.41), channel_id=1, source_target_pairs={{496,0},{0,16},{16,32},{32,48},{48,64},{64,80},{80,96},{96,112},{1... | collective-permute-start | bytes 786440 | tf_op jit(solution)/shard_map/while/body/eval_jaxpr/ppermute | solution.py:15
  189.3 8.1 %collective-permute-start = (bf16[1024,1,128]{2,0,1:T(8,128)(2,1)}, bf16[1024,1,128]{2,0,1:T(8,128)(2,1)S(1)}, u32[]{:S(2)}, u32[]{:S(2)}) collective-permute-start(bf16[1024,1,128]{2,0,1:T(8,128)(2,1)} %copy.41), channel_id=1, source_target_pairs={{496,0},{0,16},{16,32},{32,48},{48,64},{64,80},{80,96},{96,112},{1... | collective-permute-start | bytes 786440 | tf_op jit(solution)/shard_map/while/body/eval_jaxpr/ppermute | solution.py:15
  198.0 29.7 %collective-permute-start = (bf16[1024,1,128]{2,0,1:T(8,128)(2,1)}, bf16[1024,1,128]{2,0,1:T(8,128)(2,1)S(1)}, u32[]{:S(2)}, u32[]{:S(2)}) collective-permute-start(bf16[1024,1,128]{2,0,1:T(8,128)(2,1)} %copy.41), channel_id=1, source_target_pairs={{496,0},{0,16},{16,32},{32,48},{48,64},{64,80},{80,96},{96,112},{1... | collective-permute-start | bytes 786440 | tf_op jit(solution)/shard_map/while/body/eval_jaxpr/ppermute | solution.py:15
  228.5 8.2 %collective-permute-start = (bf16[1024,1,128]{2,0,1:T(8,128)(2,1)}, bf16[1024,1,128]{2,0,1:T(8,128)(2,1)S(1)}, u32[]{:S(2)}, u32[]{:S(2)}) collective-permute-start(bf16[1024,1,128]{2,0,1:T(8,128)(2,1)} %copy.41), channel_id=1, source_target_pairs={{496,0},{0,16},{16,32},{32,48},{48,64},{64,80},{80,96},{96,112},{1... | collective-permute-start | bytes 786440 | tf_op jit(solution)/shard_map/while/body/eval_jaxpr/ppermute | solution.py:15
  237.4 12.5 %collective-permute-start = (bf16[1024,1,128]{2,0,1:T(8,128)(2,1)}, bf16[1024,1,128]{2,0,1:T(8,128)(2,1)S(1)}, u32[]{:S(2)}, u32[]{:S(2)}) collective-permute-start(bf16[1024,1,128]{2,0,1:T(8,128)(2,1)} %copy.41), channel_id=1, source_target_pairs={{496,0},{0,16},{16,32},{32,48},{48,64},{64,80},{80,96},{96,112},{1... | collective-permute-start | bytes 786440 | tf_op jit(solution)/shard_map/while/body/eval_jaxpr/ppermute | solution.py:15
  250.6 20.0 %collective-permute-start = (bf16[1024,1,128]{2,0,1:T(8,128)(2,1)}, bf16[1024,1,128]{2,0,1:T(8,128)(2,1)S(1)}, u32[]{:S(2)}, u32[]{:S(2)}) collective-permute-start(bf16[1024,1,128]{2,0,1:T(8,128)(2,1)} %copy.41), channel_id=1, source_target_pairs={{496,0},{0,16},{16,32},{32,48},{48,64},{64,80},{80,96},{96,112},{1... | collective-permute-start | bytes 786440 | tf_op jit(solution)/shard_map/while/body/eval_jaxpr/ppermute | solution.py:15
  271.2 13.5 %collective-permute-start = (bf16[1024,1,128]{2,0,1:T(8,128)(2,1)}, bf16[1024,1,128]{2,0,1:T(8,128)(2,1)S(1)}, u32[]{:S(2)}, u32[]{:S(2)}) collective-permute-start(bf16[1024,1,128]{2,0,1:T(8,128)(2,1)} %copy.41), channel_id=1, source_target_pairs={{496,0},{0,16},{16,32},{32,48},{48,64},{64,80},{80,96},{96,112},{1... | collective-permute-start | bytes 786440 | tf_op jit(solution)/shard_map/while/body/eval_jaxpr/ppermute | solution.py:15
  285.4 40.2 %collective-permute-start = (bf16[1024,1,128]{2,0,1:T(8,128)(2,1)}, bf16[1024,1,128]{2,0,1:T(8,128)(2,1)S(1)}, u32[]{:S(2)}, u32[]{:S(2)}) collective-permute-start(bf16[1024,1,128]{2,0,1:T(8,128)(2,1)} %copy.41), channel_id=1, source_target_pairs={{496,0},{0,16},{16,32},{32,48},{48,64},{64,80},{80,96},{96,112},{1... | collective-permute-start | bytes 786440 | tf_op jit(solution)/shard_map/while/body/eval_jaxpr/ppermute | solution.py:15
  326.4 8.1 %collective-permute-start = (bf16[1024,1,128]{2,0,1:T(8,128)(2,1)}, bf16[1024,1,128]{2,0,1:T(8,128)(2,1)S(1)}, u32[]{:S(2)}, u32[]{:S(2)}) collective-permute-start(bf16[1024,1,128]{2,0,1:T(8,128)(2,1)} %copy.41), channel_id=1, source_target_pairs={{496,0},{0,16},{16,32},{32,48},{48,64},{64,80},{80,96},{96,112},{1... | collective-permute-start | bytes 786440 | tf_op jit(solution)/shard_map/while/body/eval_jaxpr/ppermute | solution.py:15
  335.2 18.9 %collective-permute-start = (bf16[1024,1,128]{2,0,1:T(8,128)(2,1)}, bf16[1024,1,128]{2,0,1:T(8,128)(2,1)S(1)}, u32[]{:S(2)}, u32[]{:S(2)}) collective-permute-start(bf16[1024,1,128]{2,0,1:T(8,128)(2,1)} %copy.41), channel_id=1, source_target_pairs={{496,0},{0,16},{16,32},{32,48},{48,64},{64,80},{80,96},{96,112},{1... | collective-permute-start | bytes 786440 | tf_op jit(solution)/shard_map/while/body/eval_jaxpr/ppermute | solution.py:15
  354.8 8.0 %collective-permute-start = (bf16[1024,1,128]{2,0,1:T(8,128)(2,1)}, bf16[1024,1,128]{2,0,1:T(8,128)(2,1)S(1)}, u32[]{:S(2)}, u32[]{:S(2)}) collective-permute-start(bf16[1024,1,128]{2,0,1:T(8,128)(2,1)} %copy.41), channel_id=1, source_target_pairs={{496,0},{0,16},{16,32},{32,48},{48,64},{64,80},{80,96},{96,112},{1... | collective-permute-start | bytes 786440 | tf_op jit(solution)/shard_map/while/body/eval_jaxpr/ppermute | solution.py:15
  363.5 19.0 %collective-permute-start = (bf16[1024,1,128]{2,0,1:T(8,128)(2,1)}, bf16[1024,1,128]{2,0,1:T(8,128)(2,1)S(1)}, u32[]{:S(2)}, u32[]{:S(2)}) collective-permute-start(bf16[1024,1,128]{2,0,1:T(8,128)(2,1)} %copy.41), channel_id=1, source_target_pairs={{496,0},{0,16},{16,32},{32,48},{48,64},{64,80},{80,96},{96,112},{1... | collective-permute-start | bytes 786440 | tf_op jit(solution)/shard_map/while/body/eval_jaxpr/ppermute | solution.py:15
  383.2 21.5 %collective-permute-start = (bf16[1024,1,128]{2,0,1:T(8,128)(2,1)}, bf16[1024,1,128]{2,0,1:T(8,128)(2,1)S(1)}, u32[]{:S(2)}, u32[]{:S(2)}) collective-permute-start(bf16[1024,1,128]{2,0,1:T(8,128)(2,1)} %copy.41), channel_id=1, source_target_pairs={{496,0},{0,16},{16,32},{32,48},{48,64},{64,80},{80,96},{96,112},{1... | collective-permute-start | bytes 786440 | tf_op jit(solution)/shard_map/while/body/eval_jaxpr/ppermute | solution.py:15
  405.4 13.5 %collective-permute-start = (bf16[1024,1,128]{2,0,1:T(8,128)(2,1)}, bf16[1024,1,128]{2,0,1:T(8,128)(2,1)S(1)}, u32[]{:S(2)}, u32[]{:S(2)}) collective-permute-start(bf16[1024,1,128]{2,0,1:T(8,128)(2,1)} %copy.41), channel_id=1, source_target_pairs={{496,0},{0,16},{16,32},{32,48},{48,64},{64,80},{80,96},{96,112},{1... | collective-permute-start | bytes 786440 | tf_op jit(solution)/shard_map/while/body/eval_jaxpr/ppermute | solution.py:15
  419.6 27.1 %collective-permute-start = (bf16[1024,1,128]{2,0,1:T(8,128)(2,1)}, bf16[1024,1,128]{2,0,1:T(8,128)(2,1)S(1)}, u32[]{:S(2)}, u32[]{:S(2)}) collective-permute-start(bf16[1024,1,128]{2,0,1:T(8,128)(2,1)} %copy.41), channel_id=1, source_target_pairs={{496,0},{0,16},{16,32},{32,48},{48,64},{64,80},{80,96},{96,112},{1... | collective-permute-start | bytes 786440 | tf_op jit(solution)/shard_map/while/body/eval_jaxpr/ppermute | solution.py:15
  447.4 6.7 collective-permute-start
  454.8 20.3 %collective-permute-start = (bf16[1024,1,128]{2,0,1:T(8,128)(2,1)}, bf16[1024,1,128]{2,0,1:T(8,128)(2,1)S(1)}, u32[]{:S(2)}, u32[]{:S(2)}) collective-permute-start(bf16[1024,1,128]{2,0,1:T(8,128)(2,1)} %copy.41), channel_id=1, source_target_pairs={{496,0},{0,16},{16,32},{32,48},{48,64},{64,80},{80,96},{96,112},{1... | collective-permute-start | bytes 786440 | tf_op jit(solution)/shard_map/while/body/eval_jaxpr/ppermute | solution.py:15
  475.8 13.5 %collective-permute-start = (bf16[1024,1,128]{2,0,1:T(8,128)(2,1)}, bf16[1024,1,128]{2,0,1:T(8,128)(2,1)S(1)}, u32[]{:S(2)}, u32[]{:S(2)}) collective-permute-start(bf16[1024,1,128]{2,0,1:T(8,128)(2,1)} %copy.41), channel_id=1, source_target_pairs={{496,0},{0,16},{16,32},{32,48},{48,64},{64,80},{80,96},{96,112},{1... | collective-permute-start | bytes 786440 | tf_op jit(solution)/shard_map/while/body/eval_jaxpr/ppermute | solution.py:15
  490.0 13.5 %collective-permute-start = (bf16[1024,1,128]{2,0,1:T(8,128)(2,1)}, bf16[1024,1,128]{2,0,1:T(8,128)(2,1)S(1)}, u32[]{:S(2)}, u32[]{:S(2)}) collective-permute-start(bf16[1024,1,128]{2,0,1:T(8,128)(2,1)} %copy.41), channel_id=1, source_target_pairs={{496,0},{0,16},{16,32},{32,48},{48,64},{64,80},{80,96},{96,112},{1... | collective-permute-start | bytes 786440 | tf_op jit(solution)/shard_map/while/body/eval_jaxpr/ppermute | solution.py:15
  504.2 13.5 %collective-permute-start = (bf16[1024,1,128]{2,0,1:T(8,128)(2,1)}, bf16[1024,1,128]{2,0,1:T(8,128)(2,1)S(1)}, u32[]{:S(2)}, u32[]{:S(2)}) collective-permute-start(bf16[1024,1,128]{2,0,1:T(8,128)(2,1)} %copy.41), channel_id=1, source_target_pairs={{496,0},{0,16},{16,32},{32,48},{48,64},{64,80},{80,96},{96,112},{1... | collective-permute-start | bytes 786440 | tf_op jit(solution)/shard_map/while/body/eval_jaxpr/ppermute | solution.py:15
  518.4 13.5 %collective-permute-start = (bf16[1024,1,128]{2,0,1:T(8,128)(2,1)}, bf16[1024,1,128]{2,0,1:T(8,128)(2,1)S(1)}, u32[]{:S(2)}, u32[]{:S(2)}) collective-permute-start(bf16[1024,1,128]{2,0,1:T(8,128)(2,1)} %copy.41), channel_id=1, source_target_pairs={{496,0},{0,16},{16,32},{32,48},{48,64},{64,80},{80,96},{96,112},{1... | collective-permute-start | bytes 786440 | tf_op jit(solution)/shard_map/while/body/eval_jaxpr/ppermute | solution.py:15
  532.6 13.5 %collective-permute-start = (bf16[1024,1,128]{2,0,1:T(8,128)(2,1)}, bf16[1024,1,128]{2,0,1:T(8,128)(2,1)S(1)}, u32[]{:S(2)}, u32[]{:S(2)}) collective-permute-start(bf16[1024,1,128]{2,0,1:T(8,128)(2,1)} %copy.41), channel_id=1, source_target_pairs={{496,0},{0,16},{16,32},{32,48},{48,64},{64,80},{80,96},{96,112},{1... | collective-permute-start | bytes 786440 | tf_op jit(solution)/shard_map/while/body/eval_jaxpr/ppermute | solution.py:15
  546.8 13.5 %collective-permute-start = (bf16[1024,1,128]{2,0,1:T(8,128)(2,1)}, bf16[1024,1,128]{2,0,1:T(8,128)(2,1)S(1)}, u32[]{:S(2)}, u32[]{:S(2)}) collective-permute-start(bf16[1024,1,128]{2,0,1:T(8,128)(2,1)} %copy.41), channel_id=1, source_target_pairs={{496,0},{0,16},{16,32},{32,48},{48,64},{64,80},{80,96},{96,112},{1... | collective-permute-start | bytes 786440 | tf_op jit(solution)/shard_map/while/body/eval_jaxpr/ppermute | solution.py:15
  561.1 10.1 %collective-permute-start = (bf16[1024,1,128]{2,0,1:T(8,128)(2,1)}, bf16[1024,1,128]{2,0,1:T(8,128)(2,1)S(1)}, u32[]{:S(2)}, u32[]{:S(2)}) collective-permute-start(bf16[1024,1,128]{2,0,1:T(8,128)(2,1)} %copy.41), channel_id=1, source_target_pairs={{496,0},{0,16},{16,32},{32,48},{48,64},{64,80},{80,96},{96,112},{1... | collective-permute-start | bytes 786440 | tf_op jit(solution)/shard_map/while/body/eval_jaxpr/ppermute | solution.py:15
  571.8 35.7 %collective-permute-start = (bf16[1024,1,128]{2,0,1:T(8,128)(2,1)}, bf16[1024,1,128]{2,0,1:T(8,128)(2,1)S(1)}, u32[]{:S(2)}, u32[]{:S(2)}) collective-permute-start(bf16[1024,1,128]{2,0,1:T(8,128)(2,1)} %copy.41), channel_id=1, source_target_pairs={{496,0},{0,16},{16,32},{32,48},{48,64},{64,80},{80,96},{96,112},{1... | collective-permute-start | bytes 786440 | tf_op jit(solution)/shard_map/while/body/eval_jaxpr/ppermute | solution.py:15
  608.2 7.0 collective-permute-start
  616.0 18.1 %collective-permute-start = (bf16[1024,1,128]{2,0,1:T(8,128)(2,1)}, bf16[1024,1,128]{2,0,1:T(8,128)(2,1)S(1)}, u32[]{:S(2)}, u32[]{:S(2)}) collective-permute-start(bf16[1024,1,128]{2,0,1:T(8,128)(2,1)} %copy.41), channel_id=1, source_target_pairs={{496,0},{0,16},{16,32},{32,48},{48,64},{64,80},{80,96},{96,112},{1... | collective-permute-start | bytes 786440 | tf_op jit(solution)/shard_map/while/body/eval_jaxpr/ppermute | solution.py:15
  634.7 10.4 %collective-permute-start = (bf16[1024,1,128]{2,0,1:T(8,128)(2,1)}, bf16[1024,1,128]{2,0,1:T(8,128)(2,1)S(1)}, u32[]{:S(2)}, u32[]{:S(2)}) collective-permute-start(bf16[1024,1,128]{2,0,1:T(8,128)(2,1)} %copy.41), channel_id=1, source_target_pairs={{496,0},{0,16},{16,32},{32,48},{48,64},{64,80},{80,96},{96,112},{1... | collective-permute-start | bytes 786440 | tf_op jit(solution)/shard_map/while/body/eval_jaxpr/ppermute | solution.py:15
  645.8 23.7 %collective-permute-start = (bf16[1024,1,128]{2,0,1:T(8,128)(2,1)}, bf16[1024,1,128]{2,0,1:T(8,128)(2,1)S(1)}, u32[]{:S(2)}, u32[]{:S(2)}) collective-permute-start(bf16[1024,1,128]{2,0,1:T(8,128)(2,1)} %copy.41), channel_id=1, source_target_pairs={{496,0},{0,16},{16,32},{32,48},{48,64},{64,80},{80,96},{96,112},{1... | collective-permute-start | bytes 786440 | tf_op jit(solution)/shard_map/while/body/eval_jaxpr/ppermute | solution.py:15
  670.2 38.3 %collective-permute-start = (bf16[1024,1,128]{2,0,1:T(8,128)(2,1)}, bf16[1024,1,128]{2,0,1:T(8,128)(2,1)S(1)}, u32[]{:S(2)}, u32[]{:S(2)}) collective-permute-start(bf16[1024,1,128]{2,0,1:T(8,128)(2,1)} %copy.41), channel_id=1, source_target_pairs={{496,0},{0,16},{16,32},{32,48},{48,64},{64,80},{80,96},{96,112},{1... | collective-permute-start | bytes 786440 | tf_op jit(solution)/shard_map/while/body/eval_jaxpr/ppermute | solution.py:15
  709.2 21.5 %collective-permute-start = (bf16[1024,1,128]{2,0,1:T(8,128)(2,1)}, bf16[1024,1,128]{2,0,1:T(8,128)(2,1)S(1)}, u32[]{:S(2)}, u32[]{:S(2)}) collective-permute-start(bf16[1024,1,128]{2,0,1:T(8,128)(2,1)} %copy.41), channel_id=1, source_target_pairs={{496,0},{0,16},{16,32},{32,48},{48,64},{64,80},{80,96},{96,112},{1... | collective-permute-start | bytes 786440 | tf_op jit(solution)/shard_map/while/body/eval_jaxpr/ppermute | solution.py:15
Sparse Core Ops, SparseCore 0:
  9.4 78.9 all-gather.1
where the time goes:
time: 755 us; the launch traced here: 748 us
  loops' own time  225 us (30%)
  starting transfers between devices  181 us (24%)
  waiting for transfers between devices  120 us (16%)
  local copies, waits for them, and re-layouts  95.5 us (13%)
  other arithmetic  93.7 us (12%)
  matrix products  19.3 us (3%)
  between operations  13.5 us (2%)
    another operation x32, loops' own time, run_pairs(): return lax.fori_loop(0, pair_count, one_pair, state)  223 us
    ppermute x31, starting transfers between devices, passed_along(): return lax.ppermute(block, axis, route)  175 us
    all_gather x1, waiting for transfers between devices, on_device(): lax.all_gather(w_qkv, 'team', axis=0, tiled=True)  80.1 us
    sort x32, other arithmetic, run_pairs(): jnp.argsort(jnp.where(flat_mask, 0, total_pairs) + jnp.arange(total_pairs...  64.5 us
    ppermute x31, waiting for transfers between devices, passed_along(): return lax.ppermute(block, axis, route)  28.3 us
    squeeze x36, local copies, waits for them, and re-layouts, one_pair(): lax.dynamic_index_in_dim(tiles, flat_source[pair_index], 0, keepdims=False)  26.8 us
    reduce_sum x32, other arithmetic, run_pairs(): pair_count = jnp.sum(flat_mask.astype(jnp.int32))  22.3 us
    while x31, local copies, waits for them, and re-layouts  21.5 us
  transfers between devices with their start and end apart: 33, of which 12 were waited for; matrix products, arithmetic and copies ran while one was open for 24% of the time, Pallas kernels for 0%

commit v1 on v0

v1 whole, which is shorter than its diff:
```python
import functools

import jax
import jax.numpy as jnp
from jax import lax
from jax.experimental import pallas as pl
from jax.experimental.pallas import tpu as pltpu
from jax.sharding import PartitionSpec as P

HEADS = 16
HD = 64
TILE = 128
MAXB = 8


def attend_kernel(lists, counts, q_ref, kv_hbm, out_ref, kv, sems):
    tiles = q_ref.shape[0] // TILE

    def fetch(i, j):
        return pltpu.make_async_copy(kv_hbm.at[lists[i, j]], kv.at[i, pl.ds(j * TILE, TILE)], sems.at[i])

    for i in range(tiles):
        for j in range(MAXB):
            fetch(i, j).start()

    column = lax.broadcasted_iota(jnp.int32, (TILE, MAXB * TILE), 1)

    def one_tile(i, carry):
        for j in range(MAXB):
            fetch(i, j).wait()
        rows = pl.ds(pl.multiple_of(i * TILE, TILE), TILE)
        keys = kv[i]
        scores = lax.dot_general(
            q_ref[rows, :], keys, (((1,), (1,)), ((), ())), preferred_element_type=jnp.float32
        )
        scores = jnp.where(column < counts[i] * TILE, scores * HD ** (-0.5), -1e30)
        top = jnp.max(scores, axis=-1, keepdims=True)
        weights = jnp.exp(scores - top)
        total = jnp.sum(weights, axis=-1, keepdims=True)
        summed = jnp.dot(weights.astype(jnp.bfloat16), keys, preferred_element_type=jnp.float32)
        out_ref[rows, :] = (summed / total)[:, HD:].astype(jnp.bfloat16)
        return carry

    lax.fori_loop(0, tiles, one_tile, 0)


def attend(lists, counts, q, kv):
    rows = q.shape[0]
    tiles = rows // TILE
    return pl.pallas_call(
        attend_kernel,
        grid_spec=pltpu.PrefetchScalarGridSpec(
            num_scalar_prefetch=2,
            grid=(1,),
            in_specs=[
                pl.BlockSpec((rows, 2 * HD), lambda i, *_: (0, 0)),
                pl.BlockSpec(memory_space=pl.ANY),
            ],
            out_specs=pl.BlockSpec((rows, HD), lambda i, *_: (0, 0)),
            scratch_shapes=[
                pltpu.VMEM((tiles, MAXB * TILE, 2 * HD), jnp.bfloat16),
                pltpu.SemaphoreType.DMA((tiles,)),
            ],
        ),
        out_shape=jax.ShapeDtypeStruct((rows, HD), jnp.bfloat16),
        name="attend",
    )(lists, counts, q, kv)


def on_device(tokens, norm_gain, w_qkv, block_lists, block_counts):
    xf = tokens.astype(jnp.float32)
    normed = (xf * lax.rsqrt(jnp.mean(xf * xf, axis=-1, keepdims=True) + 1e-05) * norm_gain).astype(
        jnp.bfloat16
    )
    depth = w_qkv.shape[0]
    w_head = lax.all_to_all(
        w_qkv.reshape(depth, HEADS, 3 * HD), "team", split_axis=1, concat_axis=0, tiled=True
    ).reshape(-1, 3 * HD)
    rows = lax.all_gather(normed, "team", axis=0, tiled=True)
    qkv = jnp.dot(rows, w_head, preferred_element_type=jnp.float32).astype(jnp.bfloat16)
    q = jnp.pad(qkv[:, :HD], ((0, 0), (0, HD)))
    kv = lax.all_gather(qkv[:, HD:], "seq", axis=0, tiled=True)
    return attend(block_lists, block_counts, q, kv.reshape(-1, TILE, 2 * HD))


def solution(mesh):
    in_specs = (P(("seq", "team"), None), P(), P("team", None), P("seq", None), P("seq"))
    out_specs = P("seq", "team")
    return jax.shard_map(
        on_device, mesh=mesh, in_specs=in_specs, out_specs=out_specs, check_vma=False
    )
```

time: 755 us -> 193 us (0.26)
  the two profiles are of different devices: /device:TPU:461 before, /device:TPU:1 now
where the time goes in v1:
time: 193 us
  waiting for transfers between devices  139 us (72%)
  blocking collectives  23.1 us (12%)
  between operations  13.4 us (7%)
  Pallas kernels  8.06 us (4%)
  other arithmetic  3.63 us (2%)
  local copies, waits for them, and re-layouts  3.52 us (2%)
  matrix products  2.31 us (1%)
    all_gather x1, waiting for transfers between devices, on_device(): kv = lax.all_gather(qkv[:, HD:], 'seq', axis=0, tiled=True)  92.2 us
    all_gather x1, waiting for transfers between devices, on_device(): rows = lax.all_gather(normed, 'team', axis=0, tiled=True)  46.6 us
    all_to_all x1, blocking collectives, on_device(): lax.all_to_all(w_qkv.reshape(depth, HEADS, 3 * HD), 'team', split_axis=1,...  23.1 us
    pallas_call x1, Pallas kernels, attend(): pl.pallas_call(attend_kernel, grid_spec=pltpu.PrefetchScalarGridSpec(num_...  8.06 us
  transfers between devices with their start and end apart: 2, of which 2 were waited for; matrix products, arithmetic and copies ran while one was open for 1% of the time, Pallas kernels for 0%

profile of v1, /device:TPU:1, one launch (start us, length us, event | category | flops | bytes accessed | tf_op | source)
XLA Modules:
  0.0 193.0 jit_solution(10122580055028244539)
XLA Ops:
  6.5 0.0 all-gather.3.cloned.1.call-start
  6.5 1.0 fusion
  7.6 1.7 fusion.2
  9.3 0.0 all-gather.3.cloned.1.call-update
  9.3 0.0 all-gather.5.cloned.1.call-start
  9.3 1.6 reshape.19
  11.0 0.2 copy.8
  11.1 23.1 %all_to_all.15 = bf16[64,16,192]{2,0,1:T(8,128)(2,1)S(1)} all-to-all(bf16[64,16,192]{2,0,1:T(8,128)(2,1)S(1)} %copy.8), channel_id=1, replica_groups=mesh['seq'=32,'team'=16] {'team'}, dimensions={1} | all-to-all | bytes 786432 | tf_op jit(solution)/shard_map/all_to_all | solution.py:76
  34.3 46.6 %all-gather.3.cloned.1.call-done = bf16[1024,1024]{1,0:T(8,128)(2,1)} async-done(((bf16[64,1024]{1,0:T(8,128)(2,1)}), bf16[1024,1024]{1,0:T(8,128)(2,1)}) %all-gather.3.cloned.1.call-update) | async-done | bytes 2097168 | tf_op jit(solution)/shard_map/all_gather | solution.py:79
  80.9 0.0 copy-start
  80.9 2.3 %convolution_convert_fusion = bf16[1024,192]{1,0:T(8,128)(2,1)S(1)} fusion(bf16[1024,1024]{1,0:T(8,128)(2,1)} %all-gather.3.cloned.1.call-done, bf16[1024,192]{1,0:T(8,128)(2,1)S(1)} %bitcast.9), kind=kOutput, calls=%fused_computation | convolution fusion | flops 402849792 | bytes 2883584 | tf_op jit(solution)/shard_map/dot_general | solution.py:80
  83.2 0.0 copy-done
  83.2 0.9 fusion.3
  84.1 0.0 all-gather.5.cloned.1.call-update
  84.2 92.2 %all-gather.5.cloned.1.call-done = bf16[32768,128]{1,0:T(8,128)(2,1)} async-done(((bf16[1024,128]{1,0:T(8,128)(2,1)}), bf16[32768,128]{1,0:T(8,128)(2,1)}) %all-gather.5.cloned.1.call-update) | async-done | bytes 8388624 | tf_op jit(solution)/shard_map/all_gather | solution.py:82
  176.4 8.1 %attend.1 = bf16[1024,64]{1,0:T(8,128)(2,1)} custom-call(s32[8,8]{1,0:T(8,128)} %lists.1, s32[8]{0:T(128)} %counts.1, bf16[1024,128]{1,0:T(8,128)(2,1)} %get-tuple-element.6.q_ref, bf16[256,128,128]{2,1,0:T(8,128)(2,1)} %bitcast.8), custom_call_target="tpu_custom_call" | custom-call | tf_op jit(solution)/shard_map/attend/pallas_call | solution.py:50
  184.4 1.7 copy.10
  (1 shorter events, 0.0 us)
Async XLA Ops:
  6.5 74.3 %all-gather.3.cloned.1.call-start = ((), (), s32[]{:S(2)}) async-start(), calls=%async_computation.1 | async-start | bytes 2228224 | tf_op jit(solution)/shard_map/all_gather | solution.py:79
  9.3 167.1 %all-gather.5.cloned.1.call-start = ((), (), s32[]{:S(2)}) async-start(), calls=%async_computation.2 | async-start | bytes 8650752 | tf_op jit(solution)/shard_map/all_gather | solution.py:82
  80.9 2.3 %copy-start = (pred[128]{0:T(512)(128)(4,1)S(1)}, pred[128]{0:T(512)(128)(4,1)}, u32[]{:S(2)}) copy-start(pred[128]{0:T(512)(128)(4,1)} %constant.3.clone.1) | copy-start | bytes 388
Sparse Core Ops, SparseCore 0:
  9.4 71.4 all-gather.2
  84.3 92.0 all-gather.4

commit v2 on v1

--- a/solution.py
+++ b/solution.py
@@ -1,5 +1,3 @@
-import functools
-
 import jax
 import jax.numpy as jnp
 from jax import lax
@@ -11,6 +9,238 @@
 HD = 64
 TILE = 128
 MAXB = 8
+RING = 8
+MESH = pl.DeviceIdType.MESH
+TEAM_SPACE = pltpu.VMEM
+SEQ_SPACE = pl.ANY
+
+def meet(peers):
+    barrier = pltpu.get_barrier_semaphore()
+    for peer in peers:
+        pl.semaphore_signal(barrier, inc=1, device_id=peer, device_id_type=MESH)
+    pl.semaphore_wait(barrier, len(peers))
+
+
+def team_kernel(x_ref, w_ref, out, w_out, local_sem, send_sem, recv_sem, w_send_sem, w_recv_sem):
+    me = lax.axis_index("team")
+    z, y = me // RING, lax.rem(me, RING)
+    other = 1 - z
+
+    def slot(plane, shift):
+        return plane * RING + lax.rem(y + RING + shift, RING)
+
+    right, left, across = {"team": slot(z, 1)}, {"team": slot(z, -1)}, {"team": slot(other, 0)}
+    sent = []
+
+    def send(src, index, to, arrival):
+        copy = pltpu.make_async_remote_copy(
+            src_ref=src,
+            dst_ref=out.at[index],
+            send_sem=send_sem.at[len(sent)],
+            recv_sem=recv_sem.at[arrival],
+            device_id=to,
+            device_id_type=MESH,
+        )
+        copy.start()
+        sent.append(copy)
+
+    def arrived(index, arrival):
+        pltpu.make_async_remote_copy(
+            src_ref=x_ref,
+            dst_ref=out.at[index],
+            send_sem=send_sem.at[0],
+            recv_sem=recv_sem.at[arrival],
+            device_id=right,
+            device_id_type=MESH,
+        ).wait_recv()
+
+    def w_copy(k):
+        peer = lax.rem(me + k, HEADS)
+        return pltpu.make_async_remote_copy(
+            src_ref=w_ref.at[peer],
+            dst_ref=w_out.at[me],
+            send_sem=w_send_sem.at[k],
+            recv_sem=w_recv_sem.at[k],
+            device_id={"team": peer},
+            device_id_type=MESH,
+        )
+
+    own = pltpu.make_async_copy(x_ref, out.at[me], local_sem.at[0])
+    own.start()
+    own_w = pltpu.make_async_copy(w_ref.at[me], w_out.at[me], local_sem.at[1])
+    own_w.start()
+    meet([{"team": lax.rem(me + k, HEADS)} for k in range(1, HEADS)])
+
+    send(x_ref, me, right, 0)
+    send(x_ref, me, left, 4)
+    send(x_ref, me, across, 7)
+    for k in range(1, HEADS):
+        w_copy(k).start()
+    arrived(slot(other, 0), 7)
+    send(out.at[slot(other, 0)], slot(other, 0), right, 8)
+    send(out.at[slot(other, 0)], slot(other, 0), left, 10)
+    for d in (1, 2, 3):
+        arrived(slot(z, -d), d - 1)
+        send(out.at[slot(z, -d)], slot(z, -d), right, d)
+        if d == 3:
+            send(out.at[slot(z, -3)], slot(z, -3), across, 12)
+        arrived(slot(z, d), 3 + d)
+        if d < 3:
+            send(out.at[slot(z, d)], slot(z, d), left, 4 + d)
+            arrived(slot(other, -d), 7 + d)
+            arrived(slot(other, d), 9 + d)
+            if d == 1:
+                send(out.at[slot(other, -1)], slot(other, -1), right, 9)
+                send(out.at[slot(other, 1)], slot(other, 1), left, 11)
+        else:
+            send(out.at[slot(z, 3)], slot(z, 3), across, 14)
+    arrived(slot(z, -4), 3)
+    send(out.at[slot(z, -4)], slot(z, -4), across, 13)
+    arrived(slot(other, -3), 12)
+    arrived(slot(other, 3), 14)
+    arrived(slot(other, -4), 13)
+    for k in range(1, HEADS):
+        peer = lax.rem(me + HEADS - k, HEADS)
+        pltpu.make_async_remote_copy(
+            src_ref=w_ref.at[peer],
+            dst_ref=w_out.at[peer],
+            send_sem=w_send_sem.at[k],
+            recv_sem=w_recv_sem.at[k],
+            device_id={"team": peer},
+            device_id_type=MESH,
+        ).wait_recv()
+    for k in range(1, HEADS):
+        w_copy(k).wait_send()
+    for copy in sent:
+        copy.wait_send()
+    own.wait()
+    own_w.wait()
+
+
+def team_gather(normed, w):
+    return pl.pallas_call(
+        team_kernel,
+        in_specs=[pl.BlockSpec(memory_space=TEAM_SPACE)] * 2,
+        out_specs=[pl.BlockSpec(memory_space=TEAM_SPACE)] * 2,
+        out_shape=[
+            jax.ShapeDtypeStruct((HEADS,) + normed.shape, normed.dtype),
+            jax.ShapeDtypeStruct(w.shape, w.dtype),
+        ],
+        scratch_shapes=[
+            pltpu.SemaphoreType.DMA((2,)),
+            pltpu.SemaphoreType.DMA((15,)),
+            pltpu.SemaphoreType.DMA((15,)),
+            pltpu.SemaphoreType.DMA((HEADS,)),
+            pltpu.SemaphoreType.DMA((HEADS,)),
+        ],
+        compiler_params=pltpu.CompilerParams(collective_id=0, has_side_effects=True),
+        name="team_gather",
+    )(normed, w)
+
+
+def seq_kernel(kv_ref, out, local_sem, send_sem, z_sem, x_sem, pair_sem):
+    me = lax.axis_index("seq")
+    x, z, core = me // 8, lax.rem(me // 2, 4), lax.rem(me, 2)
+    half = kv_ref.shape[0] // 2
+    shifts = (0, -1, 1, 2)
+
+    def place(xs, zs, c):
+        return lax.rem(x + 4 + xs, 4) * 8 + lax.rem(z + 4 + zs, 4) * 2 + c
+
+    z_up, z_down = {"seq": place(0, 1, core)}, {"seq": place(0, -1, core)}
+    x_up, x_down = {"seq": place(1, 0, core)}, {"seq": place(-1, 0, core)}
+    pair = {"seq": place(0, 0, 1 - core)}
+    parts = {"all": pl.ds(0, 2 * half), "low": pl.ds(0, half), "high": pl.ds(half, half)}
+    sent = []
+
+    def describe(index, part, to, arrival, send_index, first):
+        src = kv_ref if first else out.at[index]
+        return pltpu.make_async_remote_copy(
+            src_ref=src.at[parts[part]],
+            dst_ref=out.at[index, parts[part]],
+            send_sem=send_sem.at[send_index],
+            recv_sem=arrival,
+            device_id=to,
+            device_id_type=MESH,
+        )
+
+    def send(index, part, to, arrival, first=False):
+        copy = describe(index, part, to, arrival, len(sent), first)
+        copy.start()
+        sent.append(copy)
+
+    def arrived(index, part, arrival):
+        describe(index, part, pair, arrival, 0, True).wait_recv()
+
+    def spread(zi):
+        index = place(0, shifts[zi], core)
+        first = zi == 0
+        send(index, "all", x_up, x_sem.at[4 * zi], first)
+        send(index, "all", x_down, x_sem.at[4 * zi + 1], first)
+        send(index, "all", pair, pair_sem.at[4 * zi], first)
+
+    def relay(zi):
+        below, above = place(-1, shifts[zi], core), place(1, shifts[zi], core)
+        arrived(below, "all", x_sem.at[4 * zi])
+        send(below, "low", x_up, x_sem.at[4 * zi + 2])
+        send(below, "all", pair, pair_sem.at[4 * zi + 1])
+        arrived(above, "all", x_sem.at[4 * zi + 1])
+        send(above, "high", x_down, x_sem.at[4 * zi + 3])
+        send(above, "all", pair, pair_sem.at[4 * zi + 2])
+
+    def finish(zi):
+        far = place(2, shifts[zi], core)
+        arrived(far, "low", x_sem.at[4 * zi + 2])
+        arrived(far, "high", x_sem.at[4 * zi + 3])
+        send(far, "all", pair, pair_sem.at[4 * zi + 3])
+
+    own = pltpu.make_async_copy(kv_ref, out.at[me], local_sem)
+    own.start()
+    meet([z_up, z_down, x_up, x_down, pair])
+    send(me, "all", z_up, z_sem.at[0], True)
+    send(me, "all", z_down, z_sem.at[1], True)
+    spread(0)
+    relay(0)
+    arrived(place(0, -1, core), "all", z_sem.at[0])
+    send(place(0, -1, core), "low", z_up, z_sem.at[2])
+    spread(1)
+    arrived(place(0, 1, core), "all", z_sem.at[1])
+    send(place(0, 1, core), "high", z_down, z_sem.at[3])
+    spread(2)
+    finish(0)
+    relay(1)
+    arrived(place(0, 2, core), "low", z_sem.at[2])
+    arrived(place(0, 2, core), "high", z_sem.at[3])
+    spread(3)
+    relay(2)
+    finish(1)
+    finish(2)
+    relay(3)
+    finish(3)
+    for zi in range(4):
+        for xi in range(4):
+            arrived(place(shifts[xi], shifts[zi], 1 - core), "all", pair_sem.at[4 * zi + xi])
+    for copy in sent:
+        copy.wait_send()
+    own.wait()
+
+
+def seq_gather(kv):
+    return pl.pallas_call(
+        seq_kernel,
+        in_specs=[pl.BlockSpec(memory_space=SEQ_SPACE)],
+        out_specs=pl.BlockSpec(memory_space=SEQ_SPACE),
+        out_shape=jax.ShapeDtypeStruct((32,) + kv.shape, kv.dtype),
+        scratch_shapes=[
+            pltpu.SemaphoreType.DMA,
+            pltpu.SemaphoreType.DMA((36,)),
+            pltpu.SemaphoreType.DMA((4,)),
+            pltpu.SemaphoreType.DMA((16,)),
+            pltpu.SemaphoreType.DMA((16,)),
+        ],
+        compiler_params=pltpu.CompilerParams(collective_id=1, has_side_effects=True),
+        name="seq_gather",
+    )(kv)
 
 
 def attend_kernel(lists, counts, q_ref, kv_hbm, out_ref, kv, sems):
@@ -73,13 +303,12 @@
         jnp.bfloat16
     )
     depth = w_qkv.shape[0]
-    w_head = lax.all_to_all(
-        w_qkv.reshape(depth, HEADS, 3 * HD), "team", split_axis=1, concat_axis=0, tiled=True
-    ).reshape(-1, 3 * HD)
-    rows = lax.all_gather(normed, "team", axis=0, tiled=True)
+    w_blocks = w_qkv.reshape(depth, HEADS, 3 * HD).transpose(1, 0, 2)
+    rows, w_head = team_gather(normed, w_blocks)
+    rows, w_head = rows.reshape(-1, rows.shape[-1]), w_head.reshape(-1, 3 * HD)
     qkv = jnp.dot(rows, w_head, preferred_element_type=jnp.float32).astype(jnp.bfloat16)
     q = jnp.pad(qkv[:, :HD], ((0, 0), (0, HD)))
-    kv = lax.all_gather(qkv[:, HD:], "seq", axis=0, tiled=True)
+    kv = seq_gather(qkv[:, HD:])
     return attend(block_lists, block_counts, q, kv.reshape(-1, TILE, 2 * HD))
 
 

time: 193 us -> 121 us (0.63)
  the two profiles are of different devices: /device:TPU:1 before, /device:TPU:73 now
where the time goes in v2:
time: 121 us; the launch traced here: 120 us
  Pallas kernels  110 us (91%)
  local copies, waits for them, and re-layouts  4.32 us (4%)
  other arithmetic  3.64 us (3%)
  matrix products  2.39 us (2%)
    pallas_call x1, Pallas kernels, seq_gather(): pl.pallas_call(seq_kernel, in_specs=[pl.BlockSpec(memory_space=SEQ_SPACE)...  58.3 us
    pallas_call x1, Pallas kernels, team_gather(): pl.pallas_call(team_kernel, in_specs=[pl.BlockSpec(memory_space=TEAM_SPAC...  43.5 us
    pallas_call x1, Pallas kernels, attend(): pl.pallas_call(attend_kernel, grid_spec=pltpu.PrefetchScalarGridSpec(num_...  8.07 us
    reshape x2, local copies, waits for them, and re-layouts, on_device(): w_blocks = w_qkv.reshape(depth, HEADS, 3 * HD).transpose(1, 0, 2)  2.58 us

profile of v2, /device:TPU:73, one launch (start us, length us, event | category | flops | bytes accessed | tf_op | source)
XLA Modules:
  0.0 120.3 jit_solution(18098327213646909879)
XLA Ops:
  0.0 1.0 fusion
  1.0 1.7 %fusion.2.x_ref = bf16[64,1024]{1,0:T(8,128)(2,1)} fusion(bf16[64,1024]{1,0:T(8,128)(2,1)} %param.5, f32[1024]{0:T(1024)} %param.6, f32[64]{0:T(128)S(1)} %add_rsqrt_fusion), kind=kLoop, calls=%fused_computation.6 | loop fusion | flops 262144 | bytes 266496 | tf_op jit(solution)/shard_map/convert_element_type | solution.py:302
  2.7 1.6 %reshape.21 = bf16[64,16,192]{2,1,0:T(8,128)(2,1)S(1)} reshape(bf16[64,3072]{1,0:T(8,128)(2,1)} %param.7) | data formatting | bytes 786432 | tf_op jit(solution)/shard_map/reshape | solution.py:306
  4.3 1.0 copy.13
  5.3 43.5 %team_gather.1 = (bf16[16,64,1024]{2,1,0:T(8,128)(2,1)}, bf16[16,64,192]{2,1,0:T(8,128)(2,1)}) custom-call(bf16[64,1024]{1,0:T(8,128)(2,1)} %fusion.2.x_ref, bf16[16,64,192]{2,1,0:T(8,128)(2,1)} %bitcast.9), custom_call_target="tpu_custom_call" | custom-call | tf_op jit(solution)/shard_map/team_gather/pallas_call | solution.py:121
  48.8 0.0 copy-start
  48.8 2.4 %convolution_convert_fusion = bf16[1024,192]{1,0:T(8,128)(2,1)S(1)} fusion(bf16[1024,1024]{1,0:T(8,128)(2,1)} %bitcast.10, bf16[1024,192]{1,0:T(8,128)(2,1)} %bitcast.11), kind=kOutput, calls=%fused_computation | convolution fusion | flops 402849792 | bytes 2883584 | tf_op jit(solution)/shard_map/dot_general | solution.py:309
  51.2 0.0 copy-done
  51.2 0.9 fusion.3
  52.2 58.3 %seq_gather.1 = bf16[32,1024,128]{2,1,0:T(8,128)(2,1)} custom-call(bf16[1024,128]{1,0:T(8,128)(2,1)} %get-tuple-element.9.kv_ref), custom_call_target="tpu_custom_call" | custom-call | tf_op jit(solution)/shard_map/seq_gather/pallas_call | solution.py:229
  110.5 8.1 %attend.1 = bf16[1024,64]{1,0:T(8,128)(2,1)} custom-call(s32[8,8]{1,0:T(8,128)} %lists.1, s32[8]{0:T(128)} %counts.1, bf16[1024,128]{1,0:T(8,128)(2,1)} %get-tuple-element.10.q_ref, bf16[256,128,128]{2,1,0:T(8,128)(2,1)} %bitcast.8), custom_call_target="tpu_custom_call" | custom-call | tf_op jit(solution)/shard_map/attend/pallas_call | solution.py:280
  118.6 1.7 %copy.10 = bf16[1024,64]{0,1:T(8,128)(2,1)} copy(bf16[1024,64]{1,0:T(8,128)(2,1)} %attend.1) | data formatting | bytes 262144 | tf_op jit(solution)/shard_map/attend/pallas_call | solution.py:280
  (1 shorter events, 0.0 us)
Async XLA Ops:
  48.8 2.4 %copy-start = (pred[128]{0:T(512)(128)(4,1)S(1)}, pred[128]{0:T(512)(128)(4,1)}, u32[]{:S(2)}) copy-start(pred[128]{0:T(512)(128)(4,1)} %constant.3.clone.1) | copy-start | bytes 388

commit v3 on v2

--- a/solution.py
+++ b/solution.py
@@ -10,6 +10,7 @@
 TILE = 128
 MAXB = 8
 RING = 8
+WINDOW = 256
 MESH = pl.DeviceIdType.MESH
 TEAM_SPACE = pltpu.VMEM
 SEQ_SPACE = pl.ANY
@@ -21,10 +22,22 @@
     pl.semaphore_wait(barrier, len(peers))
 
 
-def team_kernel(x_ref, w_ref, out, w_out, local_sem, send_sem, recv_sem, w_send_sem, w_recv_sem):
+def team_kernel(
+    x_ref, w_ref, out, w_out, local_sem, send_sem, recv_sem, w_send_sem, w_recv_sem, p_send_sem, p_recv_sem
+):
     me = lax.axis_index("team")
     z, y = me // RING, lax.rem(me, RING)
     other = 1 - z
+    shard = lax.axis_index("seq")
+    core = lax.rem(shard, 2)
+    pair = {"seq": shard + 1 - 2 * core}
+    depth = w_ref.shape[0]
+    half = depth // 2
+    mine = pl.ds(pl.multiple_of(core * half, half), half)
+    theirs = pl.ds(pl.multiple_of((1 - core) * half, half), half)
+
+    def window(head):
+        return pl.ds(pl.multiple_of((3 * head) // 2 * 128, 128), WINDOW)
 
     def slot(plane, shift):
         return plane * RING + lax.rem(y + RING + shift, RING)
@@ -57,19 +70,41 @@
     def w_copy(k):
         peer = lax.rem(me + k, HEADS)
         return pltpu.make_async_remote_copy(
-            src_ref=w_ref.at[peer],
-            dst_ref=w_out.at[me],
+            src_ref=w_ref.at[mine, window(peer)],
+            dst_ref=w_out.at[me, mine],
             send_sem=w_send_sem.at[k],
             recv_sem=w_recv_sem.at[k],
             device_id={"team": peer},
             device_id_type=MESH,
         )
 
+    def w_arrived(k):
+        peer = lax.rem(me + HEADS - k, HEADS)
+        pltpu.make_async_remote_copy(
+            src_ref=w_ref.at[mine, window(peer)],
+            dst_ref=w_out.at[peer, mine],
+            send_sem=w_send_sem.at[k],
+            recv_sem=w_recv_sem.at[k],
+            device_id={"team": peer},
+            device_id_type=MESH,
+        ).wait_recv()
+
+    def w_pass(k, rows):
+        peer = lax.rem(me + HEADS - k, HEADS)
+        return pltpu.make_async_remote_copy(
+            src_ref=w_out.at[peer, rows],
+            dst_ref=w_out.at[peer, rows],
+            send_sem=p_send_sem.at[k],
+            recv_sem=p_recv_sem.at[k],
+            device_id=pair,
+            device_id_type=MESH,
+        )
+
     own = pltpu.make_async_copy(x_ref, out.at[me], local_sem.at[0])
     own.start()
-    own_w = pltpu.make_async_copy(w_ref.at[me], w_out.at[me], local_sem.at[1])
+    own_w = pltpu.make_async_copy(w_ref.at[:, window(me)], w_out.at[me], local_sem.at[1])
     own_w.start()
-    meet([{"team": lax.rem(me + k, HEADS)} for k in range(1, HEADS)])
+    meet([{"team": lax.rem(me + k, HEADS)} for k in range(1, HEADS)] + [pair])
 
     send(x_ref, me, right, 0)
     send(x_ref, me, left, 4)
@@ -96,21 +131,17 @@
             send(out.at[slot(z, 3)], slot(z, 3), across, 14)
     arrived(slot(z, -4), 3)
     send(out.at[slot(z, -4)], slot(z, -4), across, 13)
+    for k in range(1, HEADS):
+        w_arrived(k)
+        w_pass(k, mine).start()
     arrived(slot(other, -3), 12)
     arrived(slot(other, 3), 14)
     arrived(slot(other, -4), 13)
     for k in range(1, HEADS):
-        peer = lax.rem(me + HEADS - k, HEADS)
-        pltpu.make_async_remote_copy(
-            src_ref=w_ref.at[peer],
-            dst_ref=w_out.at[peer],
-            send_sem=w_send_sem.at[k],
-            recv_sem=w_recv_sem.at[k],
-            device_id={"team": peer},
-            device_id_type=MESH,
-        ).wait_recv()
+        w_pass(k, theirs).wait_recv()
     for k in range(1, HEADS):
         w_copy(k).wait_send()
+        w_pass(k, mine).wait_send()
     for copy in sent:
         copy.wait_send()
     own.wait()
@@ -124,12 +155,14 @@
         out_specs=[pl.BlockSpec(memory_space=TEAM_SPACE)] * 2,
         out_shape=[
             jax.ShapeDtypeStruct((HEADS,) + normed.shape, normed.dtype),
-            jax.ShapeDtypeStruct(w.shape, w.dtype),
+            jax.ShapeDtypeStruct((HEADS, w.shape[0], WINDOW), w.dtype),
         ],
         scratch_shapes=[
             pltpu.SemaphoreType.DMA((2,)),
             pltpu.SemaphoreType.DMA((15,)),
             pltpu.SemaphoreType.DMA((15,)),
+            pltpu.SemaphoreType.DMA((HEADS,)),
+            pltpu.SemaphoreType.DMA((HEADS,)),
             pltpu.SemaphoreType.DMA((HEADS,)),
             pltpu.SemaphoreType.DMA((HEADS,)),
         ],
@@ -253,22 +286,28 @@
         for j in range(MAXB):
             fetch(i, j).start()
 
-    column = lax.broadcasted_iota(jnp.int32, (TILE, MAXB * TILE), 1)
-
     def one_tile(i, carry):
         for j in range(MAXB):
             fetch(i, j).wait()
         rows = pl.ds(pl.multiple_of(i * TILE, TILE), TILE)
-        keys = kv[i]
-        scores = lax.dot_general(
-            q_ref[rows, :], keys, (((1,), (1,)), ((), ())), preferred_element_type=jnp.float32
-        )
-        scores = jnp.where(column < counts[i] * TILE, scores * HD ** (-0.5), -1e30)
-        top = jnp.max(scores, axis=-1, keepdims=True)
-        weights = jnp.exp(scores - top)
-        total = jnp.sum(weights, axis=-1, keepdims=True)
-        summed = jnp.dot(weights.astype(jnp.bfloat16), keys, preferred_element_type=jnp.float32)
-        out_ref[rows, :] = (summed / total)[:, HD:].astype(jnp.bfloat16)
+
+        def over(width):
+            keys = kv[i, : width * TILE]
+            scores = lax.dot_general(
+                keys, q_ref[rows, :], (((1,), (1,)), ((), ())), preferred_element_type=jnp.float32
+            )
+            place = lax.broadcasted_iota(jnp.int32, scores.shape, 0)
+            scores = jnp.where(place < counts[i] * TILE, scores * HD ** (-0.5), -1e30)
+            top = jnp.max(scores, axis=0, keepdims=True)
+            weights = jnp.exp(scores - top)
+            total = jnp.sum(weights, axis=0, keepdims=True)
+            summed = lax.dot_general(
+                keys, weights.astype(jnp.bfloat16), (((0,), (0,)), ((), ())), preferred_element_type=jnp.float32
+            )
+            out_ref[:, rows] = (summed[HD:] / total).astype(jnp.bfloat16)
+
+        for low, high in ((0, 1), (1, 2), (2, 4), (4, 8)):
+            pl.when((counts[i] > low) & (counts[i] <= high))(lambda high=high: over(high))
         return carry
 
     lax.fori_loop(0, tiles, one_tile, 0)
@@ -286,30 +325,38 @@
                 pl.BlockSpec((rows, 2 * HD), lambda i, *_: (0, 0)),
                 pl.BlockSpec(memory_space=pl.ANY),
             ],
-            out_specs=pl.BlockSpec((rows, HD), lambda i, *_: (0, 0)),
+            out_specs=pl.BlockSpec((HD, rows), lambda i, *_: (0, 0)),
             scratch_shapes=[
                 pltpu.VMEM((tiles, MAXB * TILE, 2 * HD), jnp.bfloat16),
                 pltpu.SemaphoreType.DMA((tiles,)),
             ],
         ),
-        out_shape=jax.ShapeDtypeStruct((rows, HD), jnp.bfloat16),
+        out_shape=jax.ShapeDtypeStruct((HD, rows), jnp.bfloat16),
         name="attend",
     )(lists, counts, q, kv)
 
 
+def norm_kernel(x_ref, gain_ref, out_ref):
+    xf = x_ref[...].astype(jnp.float32)
+    scale = lax.rsqrt(jnp.mean(xf * xf, axis=-1, keepdims=True) + 1e-05)
+    out_ref[...] = (xf * scale * gain_ref[...]).astype(jnp.bfloat16)
+
+
+def norm(tokens, gain):
+    return pl.pallas_call(
+        norm_kernel, out_shape=jax.ShapeDtypeStruct(tokens.shape, jnp.bfloat16), name="norm"
+    )(tokens, gain.reshape(1, -1))
+
+
 def on_device(tokens, norm_gain, w_qkv, block_lists, block_counts):
-    xf = tokens.astype(jnp.float32)
-    normed = (xf * lax.rsqrt(jnp.mean(xf * xf, axis=-1, keepdims=True) + 1e-05) * norm_gain).astype(
-        jnp.bfloat16
-    )
-    depth = w_qkv.shape[0]
-    w_blocks = w_qkv.reshape(depth, HEADS, 3 * HD).transpose(1, 0, 2)
-    rows, w_head = team_gather(normed, w_blocks)
-    rows, w_head = rows.reshape(-1, rows.shape[-1]), w_head.reshape(-1, 3 * HD)
+    rows, w_head = team_gather(norm(tokens, norm_gain), w_qkv)
+    rows, w_head = rows.reshape(-1, rows.shape[-1]), w_head.reshape(-1, WINDOW)
     qkv = jnp.dot(rows, w_head, preferred_element_type=jnp.float32).astype(jnp.bfloat16)
+    odd = lax.rem(lax.axis_index("team"), 2) == 1
+    qkv = jnp.where(odd, qkv[:, HD:], qkv[:, : 3 * HD])
     q = jnp.pad(qkv[:, :HD], ((0, 0), (0, HD)))
     kv = seq_gather(qkv[:, HD:])
-    return attend(block_lists, block_counts, q, kv.reshape(-1, TILE, 2 * HD))
+    return attend(block_lists, block_counts, q, kv.reshape(-1, TILE, 2 * HD)).T
 
 
 def solution(mesh):

time: 121 us -> 109 us (0.901)
  the two profiles are of different devices: /device:TPU:73 before, /device:TPU:79 now
where the time goes in v3:
time: 109 us; the launch traced here: 108 us
  Pallas kernels  105 us (96%)
  matrix products  2.38 us (2%)
  other arithmetic  1.15 us (1%)
    pallas_call x1, Pallas kernels, seq_gather(): pl.pallas_call(seq_kernel, in_specs=[pl.BlockSpec(memory_space=SEQ_SPACE)...  58 us
    pallas_call x1, Pallas kernels, team_gather(): pl.pallas_call(team_kernel, in_specs=[pl.BlockSpec(memory_space=TEAM_SPAC...  38.1 us
    pallas_call x1, Pallas kernels, attend(): pl.pallas_call(attend_kernel, grid_spec=pltpu.PrefetchScalarGridSpec(num_...  6.98 us
    dot_general x1, matrix products, on_device(): jnp.dot(rows, w_head, preferred_element_type=jnp.float32)  2.38 us

profile of v3, /device:TPU:79, one launch (start us, length us, event | category | flops | bytes accessed | tf_op | source)
XLA Modules:
  0.0 108.4 jit_solution(1277076645267922167)
XLA Ops:
  0.0 1.7 %norm.1.x_ref = bf16[64,1024]{1,0:T(8,128)(2,1)} custom-call(bf16[64,1024]{1,0:T(8,128)(2,1)} %x_ref.1, f32[1,1024]{1,0:T(1,128)} %bitcast.8), custom_call_target="tpu_custom_call" | custom-call | tf_op jit(solution)/shard_map/norm/pallas_call | solution.py:346
  1.7 38.1 %team_gather.1 = (bf16[16,64,1024]{2,1,0:T(8,128)(2,1)}, bf16[16,64,256]{2,1,0:T(8,128)(2,1)}) custom-call(bf16[64,1024]{1,0:T(8,128)(2,1)} %norm.1.x_ref, bf16[64,3072]{1,0:T(8,128)(2,1)} %w_ref.1), custom_call_target="tpu_custom_call" | custom-call | tf_op jit(solution)/shard_map/team_gather/pallas_call | solution.py:152
  39.8 0.0 copy-start
  39.8 2.4 %convolution_convert_fusion = bf16[1024,256]{1,0:T(8,128)(2,1)S(1)} fusion(bf16[1024,1024]{1,0:T(8,128)(2,1)} %bitcast.9, bf16[1024,256]{1,0:T(8,128)(2,1)} %bitcast.10), kind=kOutput, calls=%fused_computation | convolution fusion | flops 537133056 | bytes 3145728 | tf_op jit(solution)/shard_map/dot_general | solution.py:354
  42.2 0.2 slice_select_fusion
  42.5 0.0 copy-done
  42.5 0.9 fusion
  43.4 58.0 %seq_gather.1 = bf16[32,1024,128]{2,1,0:T(8,128)(2,1)} custom-call(bf16[1024,128]{1,0:T(8,128)(2,1)} %get-tuple-element.9.kv_ref), custom_call_target="tpu_custom_call" | custom-call | tf_op jit(solution)/shard_map/seq_gather/pallas_call | solution.py:262
  101.4 7.0 %attend.1 = bf16[64,1024]{1,0:T(8,128)(2,1)} custom-call(s32[8,8]{1,0:T(8,128)} %lists.1, s32[8]{0:T(128)} %counts.1, bf16[1024,128]{1,0:T(8,128)(2,1)} %get-tuple-element.10.q_ref, bf16[256,128,128]{2,1,0:T(8,128)(2,1)} %bitcast.7), custom_call_target="tpu_custom_call" | custom-call | tf_op jit(solution)/shard_map/attend/pallas_call | solution.py:319
Async XLA Ops:
  39.8 2.6 %copy-start = (pred[128]{0:T(512)(128)(4,1)S(1)}, pred[128]{0:T(512)(128)(4,1)}, u32[]{:S(2)}) copy-start(pred[128]{0:T(512)(128)(4,1)} %constant.10.clone.1) | copy-start | bytes 388

commit v4 on v3

--- a/solution.py
+++ b/solution.py
@@ -117,23 +117,24 @@
     for d in (1, 2, 3):
         arrived(slot(z, -d), d - 1)
         send(out.at[slot(z, -d)], slot(z, -d), right, d)
-        if d == 3:
-            send(out.at[slot(z, -3)], slot(z, -3), across, 12)
+        if d > 1:
+            send(out.at[slot(z, -d)], slot(z, -d), across, 9 if d == 2 else 12)
         arrived(slot(z, d), 3 + d)
         if d < 3:
             send(out.at[slot(z, d)], slot(z, d), left, 4 + d)
-            arrived(slot(other, -d), 7 + d)
-            arrived(slot(other, d), 9 + d)
-            if d == 1:
-                send(out.at[slot(other, -1)], slot(other, -1), right, 9)
-                send(out.at[slot(other, 1)], slot(other, 1), left, 11)
         else:
             send(out.at[slot(z, 3)], slot(z, 3), across, 14)
+        if d == 1:
+            arrived(slot(other, 1), 10)
+            send(out.at[slot(other, 1)], slot(other, 1), left, 11)
     arrived(slot(z, -4), 3)
     send(out.at[slot(z, -4)], slot(z, -4), across, 13)
     for k in range(1, HEADS):
         w_arrived(k)
         w_pass(k, mine).start()
+    arrived(slot(other, -1), 8)
+    arrived(slot(other, 2), 11)
+    arrived(slot(other, -2), 9)
     arrived(slot(other, -3), 12)
     arrived(slot(other, 3), 14)
     arrived(slot(other, -4), 13)
@@ -205,50 +206,72 @@
     def arrived(index, part, arrival):
         describe(index, part, pair, arrival, 0, True).wait_recv()
 
-    def spread(zi):
+    def spread(zi, part):
         index = place(0, shifts[zi], core)
-        first = zi == 0
-        send(index, "all", x_up, x_sem.at[4 * zi], first)
-        send(index, "all", x_down, x_sem.at[4 * zi + 1], first)
-        send(index, "all", pair, pair_sem.at[4 * zi], first)
+        offset = 0 if part == "low" else 1
+        send(index, part, x_up, x_sem.at[6 * zi + offset], zi == 0)
+        send(index, part, x_down, x_sem.at[6 * zi + 2 + offset], zi == 0)
+
+    def share(zi, xi):
+        send(place(shifts[xi], shifts[zi], core), "all", pair, pair_sem.at[4 * zi + xi], zi + xi == 0)
 
     def relay(zi):
         below, above = place(-1, shifts[zi], core), place(1, shifts[zi], core)
-        arrived(below, "all", x_sem.at[4 * zi])
-        send(below, "low", x_up, x_sem.at[4 * zi + 2])
-        send(below, "all", pair, pair_sem.at[4 * zi + 1])
-        arrived(above, "all", x_sem.at[4 * zi + 1])
-        send(above, "high", x_down, x_sem.at[4 * zi + 3])
-        send(above, "all", pair, pair_sem.at[4 * zi + 2])
+        arrived(below, "low", x_sem.at[6 * zi])
+        send(below, "low", x_up, x_sem.at[6 * zi + 4])
+        arrived(above, "high", x_sem.at[6 * zi + 3])
+        send(above, "high", x_down, x_sem.at[6 * zi + 5])
+
+    def settle(zi):
+        arrived(place(-1, shifts[zi], core), "high", x_sem.at[6 * zi + 1])
+        share(zi, 1)
+        arrived(place(1, shifts[zi], core), "low", x_sem.at[6 * zi + 2])
+        share(zi, 2)
 
     def finish(zi):
         far = place(2, shifts[zi], core)
-        arrived(far, "low", x_sem.at[4 * zi + 2])
-        arrived(far, "high", x_sem.at[4 * zi + 3])
-        send(far, "all", pair, pair_sem.at[4 * zi + 3])
+        arrived(far, "low", x_sem.at[6 * zi + 4])
+        arrived(far, "high", x_sem.at[6 * zi + 5])
+        share(zi, 3)
 
     own = pltpu.make_async_copy(kv_ref, out.at[me], local_sem)
     own.start()
     meet([z_up, z_down, x_up, x_down, pair])
-    send(me, "all", z_up, z_sem.at[0], True)
-    send(me, "all", z_down, z_sem.at[1], True)
-    spread(0)
+    send(me, "low", z_up, z_sem.at[0], True)
+    send(me, "high", z_down, z_sem.at[3], True)
+    spread(0, "low")
+    spread(0, "high")
+    send(me, "high", z_up, z_sem.at[1], True)
+    send(me, "low", z_down, z_sem.at[2], True)
+    share(0, 0)
     relay(0)
-    arrived(place(0, -1, core), "all", z_sem.at[0])
-    send(place(0, -1, core), "low", z_up, z_sem.at[2])
-    spread(1)
-    arrived(place(0, 1, core), "all", z_sem.at[1])
-    send(place(0, 1, core), "high", z_down, z_sem.at[3])
-    spread(2)
+    arrived(place(0, -1, core), "low", z_sem.at[0])
+    send(place(0, -1, core), "low", z_up, z_sem.at[4])
+    spread(1, "low")
+    arrived(place(0, 1, core), "high", z_sem.at[3])
+    send(place(0, 1, core), "high", z_down, z_sem.at[5])
+    spread(2, "high")
+    settle(0)
+    arrived(place(0, -1, core), "high", z_sem.at[1])
+    spread(1, "high")
+    share(1, 0)
+    arrived(place(0, 1, core), "low", z_sem.at[2])
+    spread(2, "low")
+    share(2, 0)
     finish(0)
     relay(1)
-    arrived(place(0, 2, core), "low", z_sem.at[2])
-    arrived(place(0, 2, core), "high", z_sem.at[3])
-    spread(3)
+    arrived(place(0, 2, core), "low", z_sem.at[4])
+    spread(3, "low")
+    arrived(place(0, 2, core), "high", z_sem.at[5])
+    spread(3, "high")
+    share(3, 0)
     relay(2)
+    settle(1)
+    settle(2)
+    relay(3)
     finish(1)
     finish(2)
-    relay(3)
+    settle(3)
     finish(3)
     for zi in range(4):
         for xi in range(4):
@@ -266,9 +289,9 @@
         out_shape=jax.ShapeDtypeStruct((32,) + kv.shape, kv.dtype),
         scratch_shapes=[
             pltpu.SemaphoreType.DMA,
-            pltpu.SemaphoreType.DMA((36,)),
-            pltpu.SemaphoreType.DMA((4,)),
-            pltpu.SemaphoreType.DMA((16,)),
+            pltpu.SemaphoreType.DMA((46,)),
+            pltpu.SemaphoreType.DMA((6,)),
+            pltpu.SemaphoreType.DMA((24,)),
             pltpu.SemaphoreType.DMA((16,)),
         ],
         compiler_params=pltpu.CompilerParams(collective_id=1, has_side_effects=True),
@@ -348,14 +371,38 @@
     )(tokens, gain.reshape(1, -1))
 
 
+def project_kernel(odd, x_ref, w_ref, q_ref, kv_ref):
+    qkv = jnp.dot(x_ref[...], w_ref[...], preferred_element_type=jnp.float32)
+    qkv = jnp.where(odd[0] == 1, pltpu.roll(qkv, WINDOW - HD, 1), qkv)
+    query = qkv[:, : 2 * HD]
+    lane = lax.broadcasted_iota(jnp.int32, query.shape, 1)
+    q_ref[...] = jnp.where(lane < HD, query, 0.0).astype(jnp.bfloat16)
+    kv_ref[...] = pltpu.roll(qkv, WINDOW - HD, 1)[:, : 2 * HD].astype(jnp.bfloat16)
+
+
+def project(rows, w, odd, block=256):
+    count, depth = rows.shape
+    return pl.pallas_call(
+        project_kernel,
+        grid_spec=pltpu.PrefetchScalarGridSpec(
+            num_scalar_prefetch=1,
+            grid=(count // block,),
+            in_specs=[
+                pl.BlockSpec((block, depth), lambda i, *_: (i, 0)),
+                pl.BlockSpec((depth, WINDOW), lambda i, *_: (0, 0)),
+            ],
+            out_specs=[pl.BlockSpec((block, 2 * HD), lambda i, *_: (i, 0))] * 2,
+        ),
+        out_shape=[jax.ShapeDtypeStruct((count, 2 * HD), jnp.bfloat16)] * 2,
+        name="project",
+    )(odd, rows, w)
+
+
 def on_device(tokens, norm_gain, w_qkv, block_lists, block_counts):
     rows, w_head = team_gather(norm(tokens, norm_gain), w_qkv)
-    rows, w_head = rows.reshape(-1, rows.shape[-1]), w_head.reshape(-1, WINDOW)
-    qkv = jnp.dot(rows, w_head, preferred_element_type=jnp.float32).astype(jnp.bfloat16)
-    odd = lax.rem(lax.axis_index("team"), 2) == 1
-    qkv = jnp.where(odd, qkv[:, HD:], qkv[:, : 3 * HD])
-    q = jnp.pad(qkv[:, :HD], ((0, 0), (0, HD)))
-    kv = seq_gather(qkv[:, HD:])
+    odd = lax.rem(lax.axis_index("team"), 2).astype(jnp.int32).reshape(1)
+    q, kv = project(rows.reshape(-1, rows.shape[-1]), w_head.reshape(-1, WINDOW), odd)
+    kv = seq_gather(kv)
     return attend(block_lists, block_counts, q, kv.reshape(-1, TILE, 2 * HD)).T
 
 

time: 109 us -> 105 us (0.963)
  the two profiles are of different devices: /device:TPU:79 before, /device:TPU:73 now
where the time goes in v4:
time: 105 us; the launch traced here: 104 us
  Pallas kernels  104 us (99%)
    pallas_call x1, Pallas kernels, seq_gather(): pl.pallas_call(seq_kernel, in_specs=[pl.BlockSpec(memory_space=SEQ_SPACE)...  56.4 us
    pallas_call x1, Pallas kernels, team_gather(): pl.pallas_call(team_kernel, in_specs=[pl.BlockSpec(memory_space=TEAM_SPAC...  35.7 us
    pallas_call x1, Pallas kernels, attend(): pl.pallas_call(attend_kernel, grid_spec=pltpu.PrefetchScalarGridSpec(num_...  6.16 us
    pallas_call x1, Pallas kernels, project(): pl.pallas_call(project_kernel, grid_spec=pltpu.PrefetchScalarGridSpec(num...  4.44 us

profile of v4, /device:TPU:73, one launch (start us, length us, event | category | flops | bytes accessed | tf_op | source)
XLA Modules:
  0.0 104.3 jit_solution(1443228271765163344)
XLA Ops:
  0.0 1.7 %norm.1.x_ref = bf16[64,1024]{1,0:T(8,128)(2,1)} custom-call(bf16[64,1024]{1,0:T(8,128)(2,1)} %x_ref.1, f32[1,1024]{1,0:T(1,128)} %bitcast.9), custom_call_target="tpu_custom_call" | custom-call | tf_op jit(solution)/shard_map/norm/pallas_call | solution.py:369
  1.7 35.7 %team_gather.1 = (bf16[16,64,1024]{2,1,0:T(8,128)(2,1)}, bf16[16,64,256]{2,1,0:T(8,128)(2,1)}) custom-call(bf16[64,1024]{1,0:T(8,128)(2,1)} %norm.1.x_ref, bf16[64,3072]{1,0:T(8,128)(2,1)} %w_ref.1), custom_call_target="tpu_custom_call" | custom-call | tf_op jit(solution)/shard_map/team_gather/pallas_call | solution.py:153
  37.4 4.4 %project.1 = (bf16[1024,128]{1,0:T(8,128)(2,1)}, bf16[1024,128]{1,0:T(8,128)(2,1)}) custom-call(s32[1]{0:T(128)} %bitcast.odd, bf16[1024,1024]{1,0:T(8,128)(2,1)} %bitcast.7, bf16[1024,256]{1,0:T(8,128)(2,1)} %bitcast.8), custom_call_target="tpu_custom_call" | custom-call | tf_op jit(solution)/shard_map/project/pallas_call | solution.py:385
  41.8 56.4 %seq_gather.1 = bf16[32,1024,128]{2,1,0:T(8,128)(2,1)} custom-call(bf16[1024,128]{1,0:T(8,128)(2,1)} %get-tuple-element.12.kv_ref), custom_call_target="tpu_custom_call" | custom-call | tf_op jit(solution)/shard_map/seq_gather/pallas_call | solution.py:285
  98.2 6.2 %attend.1 = bf16[64,1024]{1,0:T(8,128)(2,1)} custom-call(s32[8,8]{1,0:T(8,128)} %lists.1, s32[8]{0:T(128)} %counts.1, bf16[1024,128]{1,0:T(8,128)(2,1)} %get-tuple-element.11.q_ref, bf16[256,128,128]{2,1,0:T(8,128)(2,1)} %bitcast.6), custom_call_target="tpu_custom_call" | custom-call | tf_op jit(solution)/shard_map/attend/pallas_call | solution.py:342

commit v5 on v4

--- a/solution.py
+++ b/solution.py
@@ -12,7 +12,7 @@
 RING = 8
 WINDOW = 256
 MESH = pl.DeviceIdType.MESH
-TEAM_SPACE = pltpu.VMEM
+TEAM_SPACE = pl.ANY
 SEQ_SPACE = pl.ANY
 
 def meet(peers):
@@ -371,38 +371,14 @@
     )(tokens, gain.reshape(1, -1))
 
 
-def project_kernel(odd, x_ref, w_ref, q_ref, kv_ref):
-    qkv = jnp.dot(x_ref[...], w_ref[...], preferred_element_type=jnp.float32)
-    qkv = jnp.where(odd[0] == 1, pltpu.roll(qkv, WINDOW - HD, 1), qkv)
-    query = qkv[:, : 2 * HD]
-    lane = lax.broadcasted_iota(jnp.int32, query.shape, 1)
-    q_ref[...] = jnp.where(lane < HD, query, 0.0).astype(jnp.bfloat16)
-    kv_ref[...] = pltpu.roll(qkv, WINDOW - HD, 1)[:, : 2 * HD].astype(jnp.bfloat16)
-
-
-def project(rows, w, odd, block=256):
-    count, depth = rows.shape
-    return pl.pallas_call(
-        project_kernel,
-        grid_spec=pltpu.PrefetchScalarGridSpec(
-            num_scalar_prefetch=1,
-            grid=(count // block,),
-            in_specs=[
-                pl.BlockSpec((block, depth), lambda i, *_: (i, 0)),
-                pl.BlockSpec((depth, WINDOW), lambda i, *_: (0, 0)),
-            ],
-            out_specs=[pl.BlockSpec((block, 2 * HD), lambda i, *_: (i, 0))] * 2,
-        ),
-        out_shape=[jax.ShapeDtypeStruct((count, 2 * HD), jnp.bfloat16)] * 2,
-        name="project",
-    )(odd, rows, w)
-
-
 def on_device(tokens, norm_gain, w_qkv, block_lists, block_counts):
     rows, w_head = team_gather(norm(tokens, norm_gain), w_qkv)
-    odd = lax.rem(lax.axis_index("team"), 2).astype(jnp.int32).reshape(1)
-    q, kv = project(rows.reshape(-1, rows.shape[-1]), w_head.reshape(-1, WINDOW), odd)
-    kv = seq_gather(kv)
+    rows, w_head = rows.reshape(-1, rows.shape[-1]), w_head.reshape(-1, WINDOW)
+    qkv = jnp.dot(rows, w_head, preferred_element_type=jnp.float32).astype(jnp.bfloat16)
+    odd = lax.rem(lax.axis_index("team"), 2) == 1
+    qkv = jnp.where(odd, qkv[:, HD:], qkv[:, : 3 * HD])
+    q = jnp.pad(qkv[:, :HD], ((0, 0), (0, HD)))
+    kv = seq_gather(qkv[:, HD:])
     return attend(block_lists, block_counts, q, kv.reshape(-1, TILE, 2 * HD)).T
 
 

time: 105 us -> 102 us (0.971)
  Pallas kernels: 104 us -> 97.9 us
  matrix products: 0 us -> 2.38 us
  other arithmetic: 0 us -> 1.15 us
    pallas_call x1 -> x0, Pallas kernels: 4.44 us -> none  [project(): pl.pallas_call(project_kernel, grid_spec=pltpu.PrefetchScalarGridSpec(num...]
    dot_general x0 -> x1, matrix products: none -> 2.38 us  [on_device(): jnp.dot(rows, w_head, preferred_element_type=jnp.float32)]
where the time goes in v5:
time: 102 us
  Pallas kernels  97.9 us (96%)
  matrix products  2.38 us (2%)
  other arithmetic  1.15 us (1%)
    pallas_call x1, Pallas kernels, seq_gather(): pl.pallas_call(seq_kernel, in_specs=[pl.BlockSpec(memory_space=SEQ_SPACE)...  55.5 us
    pallas_call x1, Pallas kernels, team_gather(): pl.pallas_call(team_kernel, in_specs=[pl.BlockSpec(memory_space=TEAM_SPAC...  34.6 us
    pallas_call x1, Pallas kernels, attend(): pl.pallas_call(attend_kernel, grid_spec=pltpu.PrefetchScalarGridSpec(num_...  6.16 us
    dot_general x1, matrix products, on_device(): jnp.dot(rows, w_head, preferred_element_type=jnp.float32)  2.38 us

profile of v5, /device:TPU:73, one launch (start us, length us, event | category | flops | bytes accessed | tf_op | source)
XLA Modules:
  0.0 101.5 jit_solution(4795856371280590082)
XLA Ops:
  0.0 1.7 %norm.1.x_ref = bf16[64,1024]{1,0:T(8,128)(2,1)} custom-call(bf16[64,1024]{1,0:T(8,128)(2,1)} %x_ref.1, f32[1,1024]{1,0:T(1,128)} %bitcast.8), custom_call_target="tpu_custom_call" | custom-call | tf_op jit(solution)/shard_map/norm/pallas_call | solution.py:369
  1.7 34.6 %team_gather.1 = (bf16[16,64,1024]{2,1,0:T(8,128)(2,1)}, bf16[16,64,256]{2,1,0:T(8,128)(2,1)}) custom-call(bf16[64,1024]{1,0:T(8,128)(2,1)} %norm.1.x_ref, bf16[64,3072]{1,0:T(8,128)(2,1)} %w_ref.1), custom_call_target="tpu_custom_call" | custom-call | tf_op jit(solution)/shard_map/team_gather/pallas_call | solution.py:153
  36.3 0.0 copy-start
  36.3 2.4 %convolution_convert_fusion = bf16[1024,256]{1,0:T(8,128)(2,1)S(1)} fusion(bf16[1024,1024]{1,0:T(8,128)(2,1)} %bitcast.9, bf16[1024,256]{1,0:T(8,128)(2,1)} %bitcast.10), kind=kOutput, calls=%fused_computation | convolution fusion | flops 537133056 | bytes 3145728 | tf_op jit(solution)/shard_map/dot_general | solution.py:377
  38.7 0.2 slice_select_fusion
  38.9 0.0 copy-done
  38.9 0.9 fusion
  39.9 55.5 %seq_gather.1 = bf16[32,1024,128]{2,1,0:T(8,128)(2,1)} custom-call(bf16[1024,128]{1,0:T(8,128)(2,1)} %get-tuple-element.9.kv_ref), custom_call_target="tpu_custom_call" | custom-call | tf_op jit(solution)/shard_map/seq_gather/pallas_call | solution.py:285
  95.4 6.2 %attend.1 = bf16[64,1024]{1,0:T(8,128)(2,1)} custom-call(s32[8,8]{1,0:T(8,128)} %lists.1, s32[8]{0:T(128)} %counts.1, bf16[1024,128]{1,0:T(8,128)(2,1)} %get-tuple-element.10.q_ref, bf16[256,128,128]{2,1,0:T(8,128)(2,1)} %bitcast.7), custom_call_target="tpu_custom_call" | custom-call | tf_op jit(solution)/shard_map/attend/pallas_call | solution.py:342
Async XLA Ops:
  36.3 2.6 %copy-start = (pred[128]{0:T(512)(128)(4,1)S(1)}, pred[128]{0:T(512)(128)(4,1)}, u32[]{:S(2)}) copy-start(pred[128]{0:T(512)(128)(4,1)} %constant.10.clone.1) | copy-start | bytes 388

commit v6 on v5

--- a/solution.py
+++ b/solution.py
@@ -109,8 +109,6 @@
     send(x_ref, me, right, 0)
     send(x_ref, me, left, 4)
     send(x_ref, me, across, 7)
-    for k in range(1, HEADS):
-        w_copy(k).start()
     arrived(slot(other, 0), 7)
     send(out.at[slot(other, 0)], slot(other, 0), right, 8)
     send(out.at[slot(other, 0)], slot(other, 0), left, 10)
@@ -127,6 +125,8 @@
         if d == 1:
             arrived(slot(other, 1), 10)
             send(out.at[slot(other, 1)], slot(other, 1), left, 11)
+        for k in range(5 * d - 4, 5 * d + 1):
+            w_copy(k).start()
     arrived(slot(z, -4), 3)
     send(out.at[slot(z, -4)], slot(z, -4), across, 13)
     for k in range(1, HEADS):

time: 102 us -> 99.3 us (0.974)
  the two profiles are of different devices: /device:TPU:73 before, /device:TPU:75 now
where the time goes in v6:
time: 99.3 us; the launch traced here: 99.1 us
  Pallas kernels  95.5 us (96%)
  matrix products  2.38 us (2%)
  other arithmetic  1.15 us (1%)
    pallas_call x1, Pallas kernels, seq_gather(): pl.pallas_call(seq_kernel, in_specs=[pl.BlockSpec(memory_space=SEQ_SPACE)...  53.9 us
    pallas_call x1, Pallas kernels, team_gather(): pl.pallas_call(team_kernel, in_specs=[pl.BlockSpec(memory_space=TEAM_SPAC...  33.2 us
    pallas_call x1, Pallas kernels, attend(): pl.pallas_call(attend_kernel, grid_spec=pltpu.PrefetchScalarGridSpec(num_...  6.69 us
    dot_general x1, matrix products, on_device(): jnp.dot(rows, w_head, preferred_element_type=jnp.float32)  2.38 us

profile of v6, /device:TPU:75, one launch (start us, length us, event | category | flops | bytes accessed | tf_op | source)
XLA Modules:
  0.0 99.1 jit_solution(17417709999010505352)
XLA Ops:
  0.0 1.7 %norm.1.x_ref = bf16[64,1024]{1,0:T(8,128)(2,1)} custom-call(bf16[64,1024]{1,0:T(8,128)(2,1)} %x_ref.1, f32[1,1024]{1,0:T(1,128)} %bitcast.8), custom_call_target="tpu_custom_call" | custom-call | tf_op jit(solution)/shard_map/norm/pallas_call | solution.py:369
  1.7 33.2 %team_gather.1 = (bf16[16,64,1024]{2,1,0:T(8,128)(2,1)}, bf16[16,64,256]{2,1,0:T(8,128)(2,1)}) custom-call(bf16[64,1024]{1,0:T(8,128)(2,1)} %norm.1.x_ref, bf16[64,3072]{1,0:T(8,128)(2,1)} %w_ref.1), custom_call_target="tpu_custom_call" | custom-call | tf_op jit(solution)/shard_map/team_gather/pallas_call | solution.py:153
  34.9 0.0 copy-start
  34.9 2.4 %convolution_convert_fusion = bf16[1024,256]{1,0:T(8,128)(2,1)S(1)} fusion(bf16[1024,1024]{1,0:T(8,128)(2,1)} %bitcast.9, bf16[1024,256]{1,0:T(8,128)(2,1)} %bitcast.10), kind=kOutput, calls=%fused_computation | convolution fusion | flops 537133056 | bytes 3145728 | tf_op jit(solution)/shard_map/dot_general | solution.py:377
  37.3 0.2 slice_select_fusion
  37.5 0.0 copy-done
  37.5 0.9 fusion
  38.4 53.9 %seq_gather.1 = bf16[32,1024,128]{2,1,0:T(8,128)(2,1)} custom-call(bf16[1024,128]{1,0:T(8,128)(2,1)} %get-tuple-element.9.kv_ref), custom_call_target="tpu_custom_call" | custom-call | tf_op jit(solution)/shard_map/seq_gather/pallas_call | solution.py:285
  92.4 6.7 %attend.1 = bf16[64,1024]{1,0:T(8,128)(2,1)} custom-call(s32[8,8]{1,0:T(8,128)} %lists.1, s32[8]{0:T(128)} %counts.1, bf16[1024,128]{1,0:T(8,128)(2,1)} %get-tuple-element.10.q_ref, bf16[256,128,128]{2,1,0:T(8,128)(2,1)} %bitcast.7), custom_call_target="tpu_custom_call" | custom-call | tf_op jit(solution)/shard_map/attend/pallas_call | solution.py:342
Async XLA Ops:
  34.9 2.6 %copy-start = (pred[128]{0:T(512)(128)(4,1)S(1)}, pred[128]{0:T(512)(128)(4,1)}, u32[]{:S(2)}) copy-start(pred[128]{0:T(512)(128)(4,1)} %constant.10.clone.1) | copy-start | bytes 388
